TPU v7x, 32 devices: a whole 2x2x4 slice. The times are simulated.
32 devices in a mesh: section: 2 (over x), dp: 4 (over y, core), tensor: 4 (over z).
Axes of the slice: x: 2, y: 2, z: 4, core: 2. Of those that a mesh axis runs over, the one named last changes fastest.
Arguments:
- block_input: bfloat16 [4, 1024, 1024], P('dp'), may hold values from -6 to 6
- doc_ids: int32 [4, 1536], P('dp'), may hold values from 0 to 5, never falling along the last dimension, each value on 1 to 768 neighbouring positions
- memory: bfloat16 [2, 4, 512, 1024], P('section', 'dp'), may hold values from -6 to 6
- compressed: bfloat16 [2, 4, 512, 1024], P('section', 'dp'), may hold values from -6 to 6
- gain_attn: float32 [2, 1024], P('section'), may hold values from 0.1 to 1.9
- w_query: bfloat16 [2, 1024, 1024], P('section', None, 'tensor'), may hold values from -0.1875 to 0.1875
- w_key: bfloat16 [2, 1024, 1024], P('section', None, 'tensor'), may hold values from -0.1875 to 0.1875
- w_value: bfloat16 [2, 1024, 1024], P('section', None, 'tensor'), may hold values from -0.1875 to 0.1875
- w_out: bfloat16 [2, 1024, 1024], P('section', 'tensor'), may hold values from -1.5 to 1.5
- gain_ffn: float32 [2, 1024], P('section'), may hold values from 0.1 to 1.9
- w_up: bfloat16 [2, 1024, 4096], P('section', None, 'tensor'), may hold values from -0.1875 to 0.1875
- w_down: bfloat16 [2, 4096, 1024], P('section', 'tensor'), may hold values from -0.125 to 0.125
- w_compress: bfloat16 [2, 3, 1024, 1024], P('section', None, None, 'tensor'), may hold values from -0.109375 to 0.109375
- cotangent: bfloat16 [4, 1024, 1024], P('dp'), may hold values from -6 to 6
Outputs:
- layer_outputs: bfloat16 [2, 4, 1024, 1024], P('section', 'dp')
- input_grads: bfloat16 [2, 4, 1024, 1024], P('section', 'dp')
- grad_gain_attn: float32 [2, 1024], P('section', 'dp')
- grad_query: float32 [2, 1024, 1024], P('section', 'dp', 'tensor')
- grad_key: float32 [2, 1024, 1024], P('section', 'dp', 'tensor')
- grad_value: float32 [2, 1024, 1024], P('section', 'dp', 'tensor')
- grad_out: float32 [2, 1024, 1024], P('section', 'tensor', 'dp')
- grad_gain_ffn: float32 [2, 1024], P('section', 'dp')
- grad_up: float32 [2, 1024, 4096], P('section', 'dp', 'tensor')
- grad_down: float32 [2, 4096, 1024], P('section', 'tensor', 'dp')
- grad_compress: float32 [2, 3, 1024, 1024], P('section', None, 'dp', 'tensor')
Inputs may be any that keep to these rules, and one draw needn't show every extreme that they name: `doc_ids`: along a sequence's history the ids never fall; each document covers 1 to 768 positions, one exactly 768.
All inputs are finite; a program needn't handle non-finite values.
Results may differ from a plain program's by a relative error of at most 0.03.
Values may be sent and summed in bfloat16 or wider, within the bound.
A program may use at most 192 MiB of HBM per device.

v0:
```python
import jax
import jax.numpy as jnp
from jax import lax
from jax.sharding import PartitionSpec as P

HD = 128
SEG = 512
MEM = 512
CMEM = 512
RATE = 3
COMP_ROWS = 171
PAD = 1


epsilon = 1e-06
masked_value = -1000000000.0
split_dims = (0, 0, 0, 0, 1, 0, 0, 1, 1)


def from_behind(x, axis, by):
    size = lax.axis_size(axis)
    pairs = [(i, i + by) for i in range(size) if 0 <= i + by < size]
    return lax.ppermute(x, axis, pairs)


def normalize(row_block, gain_row):
    return (
        row_block
        * lax.rsqrt(jnp.mean(row_block * row_block, axis=-1, keepdims=True) + epsilon)
        * gain_row
    )


def contract(left_side, right_side, left_dim, right_dim):
    return lax.dot_general(
        left_side,
        right_side,
        (((left_dim,), (right_dim,)), ((), ())),
        preferred_element_type=jnp.float32,
    )


def attention_mask(key_docs, query_docs):
    key_place = jnp.concatenate([jnp.full((MEM,), -1, jnp.int32), jnp.arange(SEG, dtype=jnp.int32)])
    query_place = jnp.arange(SEG, dtype=jnp.int32)
    same_doc = key_docs[None, :] == query_docs[:, None]
    limited = same_doc & (key_place[None, :] <= query_place[:, None])
    return jnp.concatenate([jnp.ones((SEG, CMEM), bool), limited], axis=1)


def store(buffer, value, position, in_range):
    previous = lax.dynamic_index_in_dim(buffer, position, 0, keepdims=False)
    return lax.dynamic_update_index_in_dim(
        buffer, jnp.where(in_range, value, previous), position, 0
    )


def to_batches(array, sequences):
    width_last = array.shape[-1]
    return (
        array.reshape(sequences, 2, SEG, width_last)
        .transpose(1, 0, 2, 3)
        .reshape(2 * sequences, SEG, width_last)
    )


def from_batches(array, sequences):
    width_last = array.shape[-1]
    return (
        array.reshape(2, sequences, SEG, width_last)
        .transpose(1, 0, 2, 3)
        .reshape(sequences, 2 * SEG, width_last)
    )


def pack_grads(grads, groups):
    flats = [
        jnp.moveaxis(member, split_dim, 0).reshape(groups, -1)
        for member, split_dim in zip(grads, split_dims)
    ]
    return jnp.concatenate(flats, axis=1)


def unpack_grads(share, grads, groups):
    pieces = []
    offset = 0
    for member, split_dim in zip(grads, split_dims):
        moved = jnp.moveaxis(member, split_dim, 0)
        length = moved.size // groups
        piece = share[0, offset : offset + length].reshape(
            (moved.shape[0] // groups,) + moved.shape[1:]
        )
        pieces.append(jnp.moveaxis(piece, 0, split_dim))
        offset = offset + length
    return tuple(pieces)


def compress_rows(old_memory, compress_flat):
    model_width = old_memory.shape[1]
    padded = jnp.concatenate([jnp.zeros((PAD, model_width), jnp.bfloat16), old_memory]).reshape(
        COMP_ROWS, RATE * model_width
    )
    piece = jnp.dot(padded, compress_flat, preferred_element_type=jnp.float32).astype(jnp.bfloat16)
    return (padded, lax.all_gather(piece, "tensor", axis=1, tiled=True))


def batch_context(
    clamped, sequences, layer_inputs, memory_rows, compressed_rows, doc_ids, compress_flat
):
    sequence_index = clamped % sequences
    late_segment = clamped >= sequences
    history = lax.dynamic_index_in_dim(doc_ids, sequence_index, 0, keepdims=False)
    old_memory = lax.dynamic_index_in_dim(memory_rows, sequence_index, 0, keepdims=False)
    old_compressed = lax.dynamic_index_in_dim(compressed_rows, sequence_index, 0, keepdims=False)
    first_inputs = lax.dynamic_index_in_dim(layer_inputs, sequence_index, 0, keepdims=False)
    padded, fresh_rows = compress_rows(old_memory, compress_flat)
    memory_now = jnp.where(late_segment, first_inputs, old_memory)
    compressed_now = jnp.where(
        late_segment, jnp.concatenate([old_compressed[COMP_ROWS:], fresh_rows]), old_compressed
    )
    early_keys = history[: MEM + SEG]
    late_keys = history[MEM : MEM + 2 * SEG]
    key_docs = jnp.where(late_segment, late_keys, early_keys)
    query_docs = jnp.where(
        late_segment, history[MEM + SEG : MEM + 2 * SEG], history[MEM : MEM + SEG]
    )
    return (compressed_now, memory_now, key_docs, query_docs, late_segment, padded)


def attention_core(current, context, gain_attn, w_query, w_key, w_value):
    compressed_now, memory_now, key_docs, query_docs = context[:4]
    stacked = jnp.concatenate([compressed_now, memory_now, current]).astype(jnp.float32)
    row_count = stacked.shape[0]
    heads_local = w_query.shape[1] // HD
    normed = normalize(stacked, gain_attn).astype(jnp.bfloat16)
    queries = (
        jnp.dot(normed[row_count - SEG :], w_query, preferred_element_type=jnp.float32)
        .astype(jnp.bfloat16)
        .reshape(SEG, heads_local, HD)
    )
    keys_proj = (
        jnp.dot(normed, w_key, preferred_element_type=jnp.float32)
        .astype(jnp.bfloat16)
        .reshape(row_count, heads_local, HD)
    )
    values_proj = (
        jnp.dot(normed, w_value, preferred_element_type=jnp.float32)
        .astype(jnp.bfloat16)
        .reshape(row_count, heads_local, HD)
    )
    scores = jnp.einsum(
        "qhd,khd->hqk", queries, keys_proj, preferred_element_type=jnp.float32
    ) * HD ** (-0.5)
    allowed = attention_mask(key_docs, query_docs)
    scores = jnp.where(allowed[None], scores, masked_value)
    return (stacked, normed, queries, keys_proj, values_proj, scores)


def log_sum(scores):
    top_score = jnp.max(scores, axis=-1, keepdims=True)
    return top_score[..., 0] + jnp.log(jnp.sum(jnp.exp(scores - top_score), axis=-1))


def attention_mix(scores, log_total, values_proj):
    attn_probs = jnp.exp(scores - log_total[..., None])
    weights_low = attn_probs.astype(jnp.bfloat16)
    attended = jnp.einsum(
        "hqk,khd->qhd", weights_low, values_proj, preferred_element_type=jnp.float32
    ).astype(jnp.bfloat16)
    return (attn_probs, weights_low, attended)


def attention_branch(attended, w_out):
    partial_value = jnp.dot(attended.reshape(SEG, -1), w_out, preferred_element_type=jnp.float32)
    return lax.psum(partial_value.astype(jnp.bfloat16), "tensor").astype(jnp.float32)


def layer_forward(current, context, layer_weights):
    gain_attn, w_query, w_key, w_value, w_out, gain_ffn, w_up, w_down = layer_weights
    stacked, normed, queries, keys_proj, values_proj, scores = attention_core(
        current, context, gain_attn, w_query, w_key, w_value
    )
    log_total = log_sum(scores)
    ignored_probs, ignored_weights, attended = attention_mix(scores, log_total, values_proj)
    residual = current.astype(jnp.float32) + attention_branch(attended, w_out)
    normed_two = normalize(residual, gain_ffn).astype(jnp.bfloat16)
    active = jax.nn.gelu(
        jnp.dot(normed_two, w_up, preferred_element_type=jnp.float32), approximate=True
    ).astype(jnp.bfloat16)
    feed_out = lax.psum(
        jnp.dot(active, w_down, preferred_element_type=jnp.float32).astype(jnp.bfloat16), "tensor"
    ).astype(jnp.float32)
    output = (residual + feed_out).astype(jnp.bfloat16)
    return (residual, log_total, output)


def backward_batch(current, context, layer_weights, out_grad, tensor_index):
    gain_attn, w_query, w_key, w_value, w_out, gain_ffn, w_up, w_down = layer_weights
    late_segment, padded = (context[4], context[5])
    stacked, normed, queries, keys_proj, values_proj, scores = attention_core(
        current, context, gain_attn, w_query, w_key, w_value
    )
    log_total = log_sum(scores)
    attn_probs, weights_low, attended = attention_mix(scores, log_total, values_proj)
    residual = current.astype(jnp.float32) + attention_branch(attended, w_out)
    out_grad_f = out_grad.astype(jnp.float32)
    normed_two = normalize(residual, gain_ffn).astype(jnp.bfloat16)
    hidden_pre = jnp.dot(normed_two, w_up, preferred_element_type=jnp.float32)
    active, gelu_pull = jax.vjp(
        lambda argument: jax.nn.gelu(argument, approximate=True), hidden_pre
    )
    active_low = active.astype(jnp.bfloat16)
    grad_down = contract(active_low, out_grad, 0, 0)
    d_active = contract(out_grad, w_down, 1, 1)
    d_hidden = gelu_pull(d_active)[0].astype(jnp.bfloat16)
    grad_up = contract(normed_two, d_hidden, 0, 0)
    d_normed_two = lax.psum(contract(d_hidden, w_up, 1, 1).astype(jnp.bfloat16), "tensor").astype(
        jnp.float32
    )
    ignored_value, norm_pull = jax.vjp(normalize, residual, gain_ffn)
    d_resid_norm, grad_gain_ffn = norm_pull(d_normed_two)
    d_residual = out_grad_f + d_resid_norm
    d_branch = d_residual.astype(jnp.bfloat16)
    merged_heads = attended.reshape(SEG, -1)
    grad_out = contract(merged_heads, d_branch, 0, 0)
    d_attended = contract(d_branch, w_out, 1, 1).astype(jnp.bfloat16).reshape(queries.shape)
    d_values = jnp.einsum(
        "hqk,qhd->khd", weights_low, d_attended, preferred_element_type=jnp.float32
    ).astype(jnp.bfloat16)
    d_probs = jnp.einsum(
        "qhd,khd->hqk", d_attended, values_proj, preferred_element_type=jnp.float32
    )
    d_scores = (
        attn_probs * (d_probs - jnp.sum(d_probs * attn_probs, axis=-1, keepdims=True))
    ).astype(jnp.bfloat16)
    d_queries = (
        jnp.einsum("hqk,khd->qhd", d_scores, keys_proj, preferred_element_type=jnp.float32)
        * HD ** (-0.5)
    ).astype(jnp.bfloat16)
    d_keys = (
        jnp.einsum("hqk,qhd->khd", d_scores, queries, preferred_element_type=jnp.float32)
        * HD ** (-0.5)
    ).astype(jnp.bfloat16)
    row_count = normed.shape[0]
    query_flat = d_queries.reshape(SEG, -1)
    key_flat = d_keys.reshape(row_count, -1)
    value_flat = d_values.reshape(row_count, -1)
    grad_query = contract(normed[row_count - SEG :], query_flat, 0, 0)
    grad_key = contract(normed, key_flat, 0, 0)
    grad_value = contract(normed, value_flat, 0, 0)
    d_normed = contract(key_flat, w_key, 1, 1) + contract(value_flat, w_value, 1, 1)
    d_normed = d_normed.at[row_count - SEG :].add(contract(query_flat, w_query, 1, 1))
    scaled = stacked * lax.rsqrt(jnp.mean(stacked * stacked, axis=-1, keepdims=True) + epsilon)
    gain_part = jnp.sum(d_normed * scaled, axis=0)
    needed = jnp.concatenate([d_normed[CMEM - COMP_ROWS : CMEM], d_normed[row_count - SEG :]])
    needed, grad_gain_attn = (
        lax.psum(needed.astype(jnp.bfloat16), "tensor").astype(jnp.float32),
        lax.psum(gain_part.astype(jnp.bfloat16), "tensor").astype(jnp.float32),
    )
    chosen = jnp.concatenate([stacked[CMEM - COMP_ROWS : CMEM], stacked[row_count - SEG :]])
    ignored_rows, rows_pull = jax.vjp(lambda argument: normalize(argument, gain_attn), chosen)
    d_chosen = rows_pull(needed)[0]
    d_inputs = (d_residual + d_chosen[COMP_ROWS:]).astype(jnp.bfloat16)
    local_cols = padded.shape[1] // RATE // lax.axis_size("tensor")
    d_fresh = lax.dynamic_slice_in_dim(
        d_chosen[:COMP_ROWS], tensor_index * local_cols, local_cols, 1
    )
    d_fresh = jnp.where(late_segment, d_fresh, 0.0).astype(jnp.bfloat16)
    grad_compress = contract(padded, d_fresh, 0, 0).reshape(
        RATE, padded.shape[1] // RATE, local_cols
    )
    grads = (
        grad_gain_attn,
        grad_query,
        grad_key,
        grad_value,
        grad_out,
        grad_gain_ffn,
        grad_up,
        grad_down,
        grad_compress,
    )
    return (d_inputs, grads)


def shards(
    block_input,
    doc_ids,
    memory,
    compressed,
    gain_attn,
    w_query,
    w_key,
    w_value,
    w_out,
    gain_ffn,
    w_up,
    w_down,
    w_compress,
    cotangent,
):
    section_index = lax.axis_index("section")
    last_section = lax.axis_size("section") - 1
    tensor_index = lax.axis_index("tensor")
    groups = lax.axis_size("dp")
    sequences = block_input.shape[0]
    batches = 2 * sequences
    model_width = block_input.shape[2]
    layer_weights = (
        gain_attn[0],
        w_query[0],
        w_key[0],
        w_value[0],
        w_out[0],
        gain_ffn[0],
        w_up[0],
        w_down[0],
    )
    compress_flat = w_compress[0].reshape(RATE * model_width, w_compress.shape[3])
    memory_rows = memory[0]
    compressed_rows = compressed[0]
    source = to_batches(block_input, sequences)
    targets = to_batches(cotangent, sequences)
    layer_inputs = jnp.zeros((batches, SEG, model_width), jnp.bfloat16)
    layer_outputs = jnp.zeros((batches, SEG, model_width), jnp.bfloat16)
    received = jnp.zeros((SEG, model_width), jnp.bfloat16)
    tick_count = batches + last_section
    for tick_index in range(tick_count):
        batch_slot = tick_index - section_index
        in_range = (batch_slot >= 0) & (batch_slot < batches)
        clamped = jnp.clip(batch_slot, 0, batches - 1)
        current = jnp.where(section_index == 0, source[min(tick_index, batches - 1)], received)
        layer_inputs = store(layer_inputs, current, clamped, in_range)
        context = batch_context(
            clamped, sequences, layer_inputs, memory_rows, compressed_rows, doc_ids, compress_flat
        )
        residual, log_total, output = layer_forward(current, context, layer_weights)
        layer_outputs = store(layer_outputs, output, clamped, in_range)
        if tick_index < tick_count - 1:
            received = from_behind(output, "section", 1)
    input_grads = jnp.zeros((batches, SEG, model_width), jnp.bfloat16)
    incoming = jnp.zeros((SEG, model_width), jnp.bfloat16)
    totals = None
    for tick_index in range(tick_count):
        batch_slot = batches - 1 - tick_index + (last_section - section_index)
        in_range = (batch_slot >= 0) & (batch_slot < batches)
        clamped = jnp.clip(batch_slot, 0, batches - 1)
        out_grad = jnp.where(
            section_index == last_section, targets[max(batches - 1 - tick_index, 0)], incoming
        )
        current = lax.dynamic_index_in_dim(layer_inputs, clamped, 0, keepdims=False)
        context = batch_context(
            clamped, sequences, layer_inputs, memory_rows, compressed_rows, doc_ids, compress_flat
        )
        d_inputs, grads = backward_batch(current, context, layer_weights, out_grad, tensor_index)
        grads = tuple((jnp.where(in_range, member, 0.0) for member in grads))
        input_grads = store(input_grads, d_inputs, clamped, in_range)
        totals = (
            grads
            if totals is None
            else tuple((first + second for first, second in zip(totals, grads)))
        )
        if tick_index < tick_count - 1:
            incoming = from_behind(d_inputs, "section", -1)
    share = lax.psum_scatter(
        pack_grads(totals, groups).astype(jnp.bfloat16), "dp", scatter_dimension=0, tiled=True
    ).astype(jnp.float32)
    totals = unpack_grads(share, totals, groups)
    outputs_done = from_batches(layer_outputs, sequences)[None]
    grads_done = from_batches(input_grads, sequences)[None]
    return (
        outputs_done,
        grads_done,
        totals[0][None],
        totals[1][None],
        totals[2][None],
        totals[3][None],
        totals[4][None],
        totals[5][None],
        totals[6][None],
        totals[7][None],
        totals[8][None],
    )


def solution(mesh):
    return jax.shard_map(
        shards,
        mesh=mesh,
        in_specs=(
            P("dp", None, None),
            P("dp", None),
            P("section", "dp", None, None),
            P("section", "dp", None, None),
            P("section", None),
            P("section", None, "tensor"),
            P("section", None, "tensor"),
            P("section", None, "tensor"),
            P("section", "tensor", None),
            P("section", None),
            P("section", None, "tensor"),
            P("section", "tensor", None),
            P("section", None, None, "tensor"),
            P("dp", None, None),
        ),
        out_specs=(
            P("section", "dp", None, None),
            P("section", "dp", None, None),
            P("section", "dp"),
            P("section", "dp", "tensor"),
            P("section", "dp", "tensor"),
            P("section", "dp", "tensor"),
            P("section", "tensor", "dp"),
            P("section", "dp"),
            P("section", "dp", "tensor"),
            P("section", "tensor", "dp"),
            P("section", None, "dp", "tensor"),
        ),
        check_vma=False,
    )
```

profile of v0, /device:TPU:0, one launch (start us, length us, event | category | flops | bytes accessed | tf_op | source)
XLA Modules:
  0.0 1402.5 jit_solution(3030691890051331852)
XLA Ops:
  17.9 16.2 %all_gather.2 = bf16[171,1024]{1,0:T(8,128)(2,1)S(1)} all-gather(bf16[171,256]{1,0:T(8,128)(2,1)S(1)} %convolution_convert_fusion.33), channel_id=1, replica_groups=mesh['section'=2,'dp'=4,'tensor'=4] {'tensor'}, dimensions={1}, use_global_device_ids=true | all-gather | bytes 437760 | tf_op jit(solution)/shard_map/all_gather | solution.py:104
  40.3 6.2 fusion.2
  58.9 53.3 %all-reduce.23.cloned.1.call-done = bf16[512,1024]{1,0:T(8,128)(2,1)} async-done(((bf16[512,1024]{1,0:T(8,128)(2,1)}), bf16[512,1024]{1,0:T(8,128)(2,1)}) %all-reduce.23.cloned.1.call-update) | async-done | bytes 1048592 | tf_op jit(solution)/shard_map/psum | solution.py:175
  114.2 5.6 fusion.142
  119.9 51.3 %all-reduce.25.cloned.1.call-done = bf16[512,1024]{1,0:T(8,128)(2,1)} async-done(((bf16[512,1024]{1,0:T(8,128)(2,1)}), bf16[512,1024]{1,0:T(8,128)(2,1)}) %all-reduce.25.cloned.1.call-update) | async-done | bytes 1048592 | tf_op jit(solution)/shard_map/psum | solution.py:190
  173.5 3.3 bitcast_dynamic-update-slice_fusion.5
  176.8 4.3 collective-permute-start
  184.6 18.4 %collective-permute-done = bf16[512,1024]{1,0:T(8,128)(2,1)} collective-permute-done((bf16[512,1024]{1,0:T(8,128)(2,1)}, bf16[512,1024]{1,0:T(8,128)(2,1)}, u32[]{:S(2)}, u32[]{:S(2)}) %collective-permute-start) | collective-permute-done | bytes 1048608 | tf_op jit(solution)/shard_map/ppermute | solution.py:23
  207.3 6.2 fusion.5
  223.5 53.3 %all-reduce.27.cloned.1.call-done = bf16[512,1024]{1,0:T(8,128)(2,1)} async-done(((bf16[512,1024]{1,0:T(8,128)(2,1)}), bf16[512,1024]{1,0:T(8,128)(2,1)}) %all-reduce.27.cloned.1.call-update) | async-done | bytes 1048592 | tf_op jit(solution)/shard_map/psum | solution.py:175
  278.5 5.3 fusion.145
  286.2 49.0 %all-reduce.29.cloned.1.call-done = bf16[512,1024]{1,0:T(8,128)(2,1)} async-done(((bf16[512,1024]{1,0:T(8,128)(2,1)}), bf16[512,1024]{1,0:T(8,128)(2,1)}) %all-reduce.29.cloned.1.call-update) | async-done | bytes 1048592 | tf_op jit(solution)/shard_map/psum | solution.py:190
  335.2 4.2 bitcast_dynamic-update-slice_fusion.3
  339.3 4.5 collective-permute-start.1
  343.8 4.1 dot_general.395
  350.4 15.3 %collective-permute-done.1 = bf16[512,1024]{1,0:T(8,128)(2,1)} collective-permute-done((bf16[512,1024]{1,0:T(8,128)(2,1)}, bf16[512,1024]{1,0:T(8,128)(2,1)}, u32[]{:S(2)}, u32[]{:S(2)}) %collective-permute-start.1) | collective-permute-done | bytes 1048608 | tf_op jit(solution)/shard_map/ppermute | solution.py:23
  373.3 6.2 multiply_convert_fusion.5
  405.0 46.4 %all-reduce.31.cloned.1.call-done = bf16[512,1024]{1,0:T(8,128)(2,1)} async-done(((bf16[512,1024]{1,0:T(8,128)(2,1)}), bf16[512,1024]{1,0:T(8,128)(2,1)}) %all-reduce.31.cloned.1.call-update) | async-done | bytes 1048592 | tf_op jit(solution)/shard_map/psum | solution.py:175
  453.4 3.0 fusion.116
  462.6 5.5 fusion.336
  468.1 3.4 fusion.179
  471.5 41.9 %all-reduce.33.cloned.1.call-done = bf16[512,1024]{1,0:T(8,128)(2,1)} async-done(((bf16[512,1024]{1,0:T(8,128)(2,1)}), bf16[512,1024]{1,0:T(8,128)(2,1)}) %all-reduce.33.cloned.1.call-update) | async-done | bytes 1048592 | tf_op jit(solution)/shard_map/psum | solution.py:217
  513.4 3.5 fusion.40
  517.0 3.2 fusion.88
  536.8 5.5 multiply_reduce_fusion.2
  542.3 12.7 multiply_convert_fusion.1
  557.5 4.0 convolution_convert_fusion.9
  576.0 3.1 fusion.11
  584.2 3.1 fusion.14
  594.3 2.7 fusion.170
  597.0 2.7 convolution_convert_fusion.21
  599.7 82.1 %all-reduce.45.cloned.1.call-done = (bf16[683,1024]{1,0:T(8,128)(2,1)}, bf16[512,1024]{1,0:T(8,128)(2,1)}) async-done(((bf16[683,1024]{1,0:T(8,128)(2,1)}, bf16[512,1024]{1,0:T(8,128)(2,1)}), (bf16[683,1024]{1,0:T(8,128)(2,1)}, bf16[512,1024]{1,0:T(8,128)(2,1)})) %all-reduce.45.cloned.1.call-update) | async-done | bytes 2447376 | tf_op jit(solution)/shard_map/psum | solution.py:257
  681.9 3.1 multiply_reduce_fusion.14
  694.2 21.9 %collective-permute-done.2 = bf16[512,1024]{1,0:T(8,128)(2,1)S(1)} collective-permute-done((bf16[512,1024]{1,0:T(8,128)(2,1)S(1)}, bf16[512,1024]{1,0:T(8,128)(2,1)S(1)}, u32[]{:S(2)}, u32[]{:S(2)}) %collective-permute-start.2) | collective-permute-done | bytes 1048608 | tf_op jit(solution)/shard_map/ppermute | solution.py:23
  724.5 3.4 convolution_select_fusion.2
  733.9 38.4 %all-reduce.35.cloned.1.call-done = bf16[512,1024]{1,0:T(8,128)(2,1)} async-done(((bf16[512,1024]{1,0:T(8,128)(2,1)}), bf16[512,1024]{1,0:T(8,128)(2,1)}) %all-reduce.35.cloned.1.call-update) | async-done | bytes 1048592 | tf_op jit(solution)/shard_map/psum | solution.py:217
  775.0 2.8 fusion.89
  796.2 5.1 fusion.337
  801.3 3.4 fusion.180
  810.6 5.9 multiply_reduce_fusion.1
  816.6 77.2 %all-reduce.43.cloned.1.call-done = (bf16[683,1024]{1,0:T(8,128)(2,1)}, bf16[512,1024]{1,0:T(8,128)(2,1)}) async-done(((bf16[683,1024]{1,0:T(8,128)(2,1)}, bf16[512,1024]{1,0:T(8,128)(2,1)}), (bf16[683,1024]{1,0:T(8,128)(2,1)}, bf16[512,1024]{1,0:T(8,128)(2,1)})) %all-reduce.43.cloned.1.call-update) | async-done | bytes 2447376 | tf_op jit(solution)/shard_map/psum | solution.py:257
  893.8 3.1 multiply_reduce_fusion.12
  906.6 21.2 %collective-permute-done.3 = bf16[512,1024]{1,0:T(8,128)(2,1)S(1)} collective-permute-done((bf16[512,1024]{1,0:T(8,128)(2,1)S(1)}, bf16[512,1024]{1,0:T(8,128)(2,1)S(1)}, u32[]{:S(2)}, u32[]{:S(2)}) %collective-permute-start.3) | collective-permute-done | bytes 1048608 | tf_op jit(solution)/shard_map/ppermute | solution.py:23
  933.9 2.9 convolution_select_fusion.4
  940.8 5.8 add_convert_fusion.1
  946.6 4.6 reshape.624
  951.2 6.4 add_convert_fusion
  957.6 4.5 reshape.625
  962.1 56.1 %all-reduce.41.cloned.1.call-done = (bf16[512,1024]{1,0:T(8,128)(2,1)}, bf16[512,1024]{1,0:T(8,128)(2,1)}) async-done(((bf16[512,1024]{1,0:T(8,128)(2,1)}, bf16[512,1024]{1,0:T(8,128)(2,1)}), (bf16[512,1024]{1,0:T(8,128)(2,1)}, bf16[512,1024]{1,0:T(8,128)(2,1)})) %all-reduce.41.cloned.1.call-update) | async-done | bytes 2097168 | tf_op jit(solution)/shard_map/psum | solution.py:175
  1024.0 5.9 convolution_convert_fusion
  1043.9 6.1 multiply_reduce_fusion
  1053.4 3.6 fusion.168
  1059.2 5.3 fusion.148
  1064.6 4.4 fusion.167
  1076.0 10.1 all-reduce.5
  1100.9 84.8 %all-reduce.39.cloned.1.call-done = (bf16[512,1024]{1,0:T(8,128)(2,1)}, bf16[683,1024]{1,0:T(8,128)(2,1)}) async-done(((bf16[512,1024]{1,0:T(8,128)(2,1)}, bf16[683,1024]{1,0:T(8,128)(2,1)}), (bf16[512,1024]{1,0:T(8,128)(2,1)}, bf16[683,1024]{1,0:T(8,128)(2,1)})) %all-reduce.39.cloned.1.call-update) | async-done | bytes 2447376 | tf_op jit(solution)/shard_map/psum | solution.py:190
  1185.8 3.1 multiply_reduce_fusion.10
  1194.7 2.7 copy.90
  1197.4 4.1 reshape.626
  1212.8 135.6 %all-reduce.37.cloned.1.call-done = bf16[4,983552]{1,0:T(4,128)(2,1)} async-done(((bf16[4,983552]{1,0:T(4,128)(2,1)}), bf16[4,983552]{1,0:T(4,128)(2,1)}) %all-reduce.37.cloned.1.call-update) | async-done | bytes 7868432
  1348.4 8.0 dynamic-slice_convert_fusion
  1356.9 9.2 slice_reduce_fusion.2
  1366.2 3.5 slice_reduce_fusion.3
  1369.6 12.3 slice_reduce_fusion
  (648 shorter events, 291.2 us)
Async XLA Ops:
  7.2 107.0 %copy-start = (bf16[1,1024,1024]{2,1,0:T(8,128)(2,1)S(1)}, bf16[1,1024,1024]{2,1,0:T(8,128)(2,1)}, u32[]{:S(2)}) copy-start(bf16[1,1024,1024]{2,1,0:T(8,128)(2,1)} %param.30) | copy-start | bytes 6291460
  7.2 105.1 %all-reduce.23.cloned.1.call-start = ((), (), s32[]{:S(2)}) async-start(), calls=%async_computation | async-start | bytes 2097152 | tf_op jit(solution)/shard_map/psum | solution.py:175
  17.9 19.6 %copy-start.70 = (bf16[1,1,512,1024]{3,2,1,0:T(8,128)(2,1)S(1)}, bf16[1,1,512,1024]{3,2,1,0:T(8,128)(2,1)}, u32[]{:S(2)}) copy-start(bf16[1,1,512,1024]{3,2,1,0:T(8,128)(2,1)} %param.22) | copy-start | bytes 3145732
  39.3 7.2 copy-start.12
  39.3 168.0 %copy-start.17 = (bf16[512,1024]{1,0:T(8,128)(2,1)}, bf16[512,1024]{1,0:T(8,128)(2,1)S(1)}, u32[]{:S(2)}) copy-start(bf16[512,1024]{1,0:T(8,128)(2,1)S(1)} %get-tuple-element.118) | copy-start | bytes 3145732
  40.2 6.2 copy-start.107
  40.3 6.7 copy-start.101
  57.0 57.3 %copy-start.166 = (f32[1,1024]{1,0:T(1,128)S(1)}, f32[1,1024]{1,0:T(1,128)}, u32[]{:S(2)}) copy-start(f32[1,1024]{1,0:T(1,128)} %param.29) | copy-start | bytes 12292
  58.5 112.7 %all-reduce.25.cloned.1.call-start = ((), (), s32[]{:S(2)}) async-start(), calls=%async_computation.1 | async-start | bytes 2097152 | tf_op jit(solution)/shard_map/psum | solution.py:190
  119.9 157.0 %all-reduce.27.cloned.1.call-start = ((), (), s32[]{:S(2)}) async-start(), calls=%async_computation.2 | async-start | bytes 2097152 | tf_op jit(solution)/shard_map/psum | solution.py:175
  176.8 26.2 %collective-permute-start = (bf16[512,1024]{1,0:T(8,128)(2,1)}, bf16[512,1024]{1,0:T(8,128)(2,1)}, u32[]{:S(2)}, u32[]{:S(2)}) collective-permute-start(bf16[512,1024]{1,0:T(8,128)(2,1)} %get-tuple-element.111), channel_id=1, source_target_pairs={{0,16},{1,17},{2,18},{3,19},{4,20},{5,21},{6,22},{7,23},{8,24},{9,... | collective-permute-start | bytes 3145736 | tf_op jit(solution)/shard_map/ppermute | solution.py:23
  183.2 19.8 %copy-start.117 = (bf16[1,1024,1024]{2,1,0:T(8,128)(2,1)S(1)}, bf16[1,1024,1024]{2,1,0:T(8,128)(2,1)}, u32[]{:S(2)}) copy-start(bf16[1,1024,1024]{2,1,0:T(8,128)(2,1)} %param.20) | copy-start | bytes 6291460
  184.6 20.1 %copy-start.71 = (bf16[1,1,512,1024]{3,2,1,0:T(8,128)(2,1)S(1)}, bf16[1,1,512,1024]{3,2,1,0:T(8,128)(2,1)}, u32[]{:S(2)}) copy-start(bf16[1,1,512,1024]{3,2,1,0:T(8,128)(2,1)} %param.22) | copy-start | bytes 3145732
  207.3 6.2 copy-start.108
  207.3 6.7 copy-start.102
  221.8 55.1 %copy-start.64 = (bf16[512,1024]{1,0:T(8,128)(2,1)S(1)}, bf16[512,1024]{1,0:T(8,128)(2,1)}, u32[]{:S(2)}) copy-start(bf16[512,1024]{1,0:T(8,128)(2,1)} %copy-done.63) | copy-start | bytes 3145732
  223.3 111.9 %all-reduce.29.cloned.1.call-start = ((), (), s32[]{:S(2)}) async-start(), calls=%async_computation.3 | async-start | bytes 2097152 | tf_op jit(solution)/shard_map/psum | solution.py:190
  283.9 167.5 %all-reduce.31.cloned.1.call-start = ((), (), s32[]{:S(2)}) async-start(), calls=%async_computation.4 | async-start | bytes 2097152 | tf_op jit(solution)/shard_map/psum | solution.py:175
  339.3 8.6 copy-start.153
  339.3 26.3 %collective-permute-start.1 = (bf16[512,1024]{1,0:T(8,128)(2,1)}, bf16[512,1024]{1,0:T(8,128)(2,1)}, u32[]{:S(2)}, u32[]{:S(2)}) collective-permute-start(bf16[512,1024]{1,0:T(8,128)(2,1)} %get-tuple-element.107), channel_id=1, source_target_pairs={{0,16},{1,17},{2,18},{3,19},{4,20},{5,21},{6,22},{7,23},{8,24},{9,... | collective-permute-start | bytes 3145736 | tf_op jit(solution)/shard_map/ppermute | solution.py:23
  348.9 16.7 %copy-start.118 = (bf16[1,1024,1024]{2,1,0:T(8,128)(2,1)S(1)}, bf16[1,1024,1024]{2,1,0:T(8,128)(2,1)}, u32[]{:S(2)}) copy-start(bf16[1,1024,1024]{2,1,0:T(8,128)(2,1)} %param.20) | copy-start | bytes 6291460
  370.5 12.0 copy-start.6
  370.8 8.7 copy-start.41
  370.8 11.7 copy-start.50
  370.8 15.4 %copy-start.54 = (bf16[512,1024]{1,0:T(8,128)(2,1)}, bf16[512,1024]{1,0:T(8,128)(2,1)S(1)}, u32[]{:S(2)}) copy-start(bf16[512,1024]{1,0:T(8,128)(2,1)S(1)} %get-tuple-element.115) | copy-start | bytes 3145732
  373.3 6.2 copy-start.109
  373.3 6.7 copy-start.103
  381.5 7.9 copy-start.139
  382.5 10.7 copy-start.171
  397.9 115.5 %all-reduce.33.cloned.1.call-start = ((), (), s32[]{:S(2)}) async-start(), calls=%async_computation.5 | async-start | bytes 2097152 | tf_op jit(solution)/shard_map/psum | solution.py:217
  404.3 138.0 %copy-start.179 = (f32[1536]{0:T(1024)}, f32[1536]{0:T(1024)S(1)}, u32[]{:S(2)}) copy-start(f32[1536]{0:T(1024)S(1)} %add_rsqrt_fusion) | copy-start | bytes 18436
  462.1 219.8 %all-reduce.45.cloned.1.call-start = ((), (), s32[]{:S(2)}) async-start(), calls=%async_computation.11 | async-start | bytes 4915200 | tf_op jit(solution)/shard_map/psum | solution.py:257
  513.4 8.6 slice-start.4
  524.8 8.2 copy-start.173
  584.2 188.1 %all-reduce.35.cloned.1.call-start = ((), (), s32[]{:S(2)}) async-start(), calls=%async_computation.6 | async-start | bytes 2097152 | tf_op jit(solution)/shard_map/psum | solution.py:217
  587.4 9.6 copy-start.1
  587.4 6.6 slice-start.8
  689.5 26.6 %collective-permute-start.2 = (bf16[512,1024]{1,0:T(8,128)(2,1)S(1)}, bf16[512,1024]{1,0:T(8,128)(2,1)S(1)}, u32[]{:S(2)}, u32[]{:S(2)}) collective-permute-start(bf16[512,1024]{1,0:T(8,128)(2,1)S(1)} %get-tuple-element.103), channel_id=1, source_target_pairs={{16,0},{17,1},{18,2},{19,3},{20,4},{21,5},{22,6},{23,7},{24,8},{25... | collective-permute-start | bytes 3145736 | tf_op jit(solution)/shard_map/ppermute | solution.py:23
  692.8 23.3 %copy-start.115 = (bf16[1,1024,1024]{2,1,0:T(8,128)(2,1)S(1)}, bf16[1,1024,1024]{2,1,0:T(8,128)(2,1)}, u32[]{:S(2)}) copy-start(bf16[1,1024,1024]{2,1,0:T(8,128)(2,1)} %param.33) | copy-start | bytes 6291460
  694.2 24.4 %copy-start.190 = (f32[512,1024]{1,0:T(8,128)}, f32[512,1024]{1,0:T(8,128)S(1)}, u32[]{:S(2)}) copy-start(f32[512,1024]{1,0:T(8,128)S(1)} %fusion.112) | copy-start | bytes 6291460
  694.2 22.0 %copy-start.185 = (bf16[1,1024,1024]{2,1,0:T(8,128)(2,1)S(1)}, bf16[1,1024,1024]{2,1,0:T(8,128)(2,1)}, u32[]{:S(2)}) copy-start(bf16[1,1024,1024]{2,1,0:T(8,128)(2,1)} %param.31) | copy-start | bytes 6291460
  721.9 171.9 %all-reduce.43.cloned.1.call-start = ((), (), s32[]{:S(2)}) async-start(), calls=%async_computation.10 | async-start | bytes 4915200 | tf_op jit(solution)/shard_map/psum | solution.py:257
  724.5 6.8 copy-start.82
  772.3 6.8 slice-start.2
  781.6 8.4 copy-start.175
  796.1 222.2 %all-reduce.41.cloned.1.call-start = ((), (), s32[]{:S(2)}) async-start(), calls=%async_computation.9 | async-start | bytes 4194304 | tf_op jit(solution)/shard_map/psum | solution.py:175
  804.7 5.9 slice-start.6
  816.5 80.4 %copy-start.88 = (f32[171,1024]{1,0:T(8,128)S(1)}, f32[171,1024]{1,0:T(8,128)}, u32[]{:S(2)}) copy-start(f32[171,1024]{1,0:T(8,128)} %slice.302) | copy-start | bytes 2101252
  900.9 26.9 %collective-permute-start.3 = (bf16[512,1024]{1,0:T(8,128)(2,1)S(1)}, bf16[512,1024]{1,0:T(8,128)(2,1)S(1)}, u32[]{:S(2)}, u32[]{:S(2)}) collective-permute-start(bf16[512,1024]{1,0:T(8,128)(2,1)S(1)} %get-tuple-element.101), channel_id=1, source_target_pairs={{16,0},{17,1},{18,2},{19,3},{20,4},{21,5},{22,6},{23,7},{24,8},{25... | collective-permute-start | bytes 3145736 | tf_op jit(solution)/shard_map/ppermute | solution.py:23
  905.2 22.6 %copy-start.116 = (bf16[1,1024,1024]{2,1,0:T(8,128)(2,1)S(1)}, bf16[1,1024,1024]{2,1,0:T(8,128)(2,1)}, u32[]{:S(2)}) copy-start(bf16[1,1024,1024]{2,1,0:T(8,128)(2,1)} %param.33) | copy-start | bytes 6291460
  906.5 23.7 %copy-start.195 = (f32[512,1024]{1,0:T(8,128)}, f32[512,1024]{1,0:T(8,128)S(1)}, u32[]{:S(2)}) copy-start(f32[512,1024]{1,0:T(8,128)S(1)} %fusion.108) | copy-start | bytes 6291460
  906.5 21.3 %copy-start.186 = (bf16[1,1024,1024]{2,1,0:T(8,128)(2,1)S(1)}, bf16[1,1024,1024]{2,1,0:T(8,128)(2,1)}, u32[]{:S(2)}) copy-start(bf16[1,1024,1024]{2,1,0:T(8,128)(2,1)} %param.31) | copy-start | bytes 6291460
  933.6 252.2 %all-reduce.39.cloned.1.call-start = ((), (), s32[]{:S(2)}) async-start(), calls=%async_computation.8 | async-start | bytes 4915200 | tf_op jit(solution)/shard_map/psum | solution.py:190
  933.9 6.9 copy-start.80
  1022.0 7.9 slice-start
  1024.0 5.9 copy-start.168
  1043.9 6.2 copy-start.59
  1043.9 6.2 copy-start.126
  1069.0 7.0 copy-start.182
  1069.0 17.1 %copy-start.181 = (f32[1024]{0:T(1024)S(1)}, f32[1024]{0:T(1024)}, u32[]{:S(2)}) copy-start(f32[1024]{0:T(1024)} %get-tuple-element.75) | copy-start | bytes 12292
  1089.4 259.0 %all-reduce.37.cloned.1.call-start = ((), (), s32[]{:S(2)}) async-start(), calls=%async_computation.7 | async-start | bytes 15736832
  1089.4 6.3 copy-start.154
  1089.4 7.8 copy-start.85
  1387.1 7.1 copy-start.135
  (158 other events, 432.0 us)
Sparse Core Ops, SparseCore 0:
  58.6 53.6 all-reduce.22
  120.0 51.1 all-reduce.24
  223.4 53.3 all-reduce.26
  284.0 51.1 all-reduce.28
  398.0 53.3 all-reduce.30
  462.2 51.1 all-reduce.32
  584.3 97.5 all-reduce.44
  722.0 50.2 all-reduce.34
  796.2 97.5 all-reduce.42
  933.7 84.5 all-reduce.40
  1089.5 96.2 all-reduce.38
  1204.2 144.0 all-reduce.36
where the time goes:
time: 1410 us; the launch traced here: 1400 us
  waiting for transfers between devices  847 us (60%)
  matrix products  191 us (14%)
  local copies, waits for them, and re-layouts  155 us (11%)
  other arithmetic  153 us (11%)
  blocking collectives  26.3 us (2%)
  between operations  17.1 us (1%)
    psum x4, waiting for transfers between devices, attention_branch(): lax.psum(partial_value.astype(jnp.bfloat16), 'tensor').astype(jnp.float32)  209 us
    psum x3, waiting for transfers between devices, layer_forward(): lax.psum(jnp.dot(active, w_down, preferred_element_type=jnp.float32).asty...  185 us
    psum x2, waiting for transfers between devices, backward_batch(): lax.psum(needed.astype(jnp.bfloat16), 'tensor').astype(jnp.float32)  159 us
    unnamed x13, waiting for transfers between devices  136 us
    dot_general x39, matrix products, contract(): lax.dot_general(left_side, right_side, (((left_dim,), (right_dim,)), ((),...  86.8 us
    psum x2, waiting for transfers between devices, backward_batch(): lax.psum(contract(d_hidden, w_up, 1, 1).astype(jnp.bfloat16), 'tensor')  80.4 us
    ppermute x4, waiting for transfers between devices, from_behind(): return lax.ppermute(x, axis, pairs)  76.7 us
    unnamed x423, local copies, waits for them, and re-layouts  52.7 us
  transfers between devices with their start and end apart: 16, of which 16 were waited for; matrix products, arithmetic and copies ran while one was open for 9% of the time, Pallas kernels for 0%

commit v1 on v0

v1 whole, which is shorter than its diff:
```python
import functools

import jax
import jax.numpy as jnp
from jax import lax
from jax.experimental import pallas as pl
from jax.experimental.pallas import tpu as pltpu
from jax.sharding import PartitionSpec as P

HD = 128
SEG = 512
MEM = 512
CMEM = 512
RATE = 3
COMP_ROWS = 171
PAD = 1
OLD_ROWS = CMEM - COMP_ROWS
CHUNKS = 4
ROWS = SEG // CHUNKS
FRESH_START = OLD_ROWS // 16 * 16

epsilon = 1e-06
masked_value = -1000000000.0
MESH = pl.DeviceIdType.MESH
f32 = jnp.float32
bf16 = jnp.bfloat16
GELU_A = 0.7978845608028654
GELU_B = 0.044715


def inverse_rms(rows):
    return lax.rsqrt(jnp.mean(rows * rows, axis=-1, keepdims=True) + epsilon)


def rms_pull(grad, rows, gain):
    scale = inverse_rms(rows)
    scaled_grad = grad * gain
    inner = jnp.mean(scaled_grad * rows, axis=-1, keepdims=True)
    return scale * (scaled_grad - rows * (scale * scale * inner))


def gelu(x):
    return 0.5 * x * (1.0 + jnp.tanh(GELU_A * (x + GELU_B * x * x * x)))


def gelu_slope(x):
    square = x * x
    bend = jnp.tanh(GELU_A * (x + GELU_B * x * square))
    return 0.5 * (1.0 + bend) + 0.5 * x * (1.0 - bend * bend) * GELU_A * (
        1.0 + 3.0 * GELU_B * square
    )


def dot_nn(a, b):
    return lax.dot_general(a, b, (((1,), (0,)), ((), ())), preferred_element_type=f32)


def dot_nt(a, b):
    return lax.dot_general(a, b, (((1,), (1,)), ((), ())), preferred_element_type=f32)


def dot_tn(a, b):
    return lax.dot_general(a, b, (((0,), (0,)), ((), ())), preferred_element_type=f32)


def greet(n, with_peer):
    me = lax.axis_index("tensor")
    barrier = pltpu.get_barrier_semaphore()
    for step in (-1, 1):
        other = me + step

        @pl.when((other >= 0) & (other < n))
        def _():
            pl.semaphore_signal(barrier, inc=1, device_id={"tensor": other}, device_id_type=MESH)

    if with_peer:
        peer = 1 - lax.axis_index("section")
        pl.semaphore_signal(barrier, inc=1, device_id={"section": peer}, device_id_type=MESH)
    extra = 1 if with_peer else 0
    pl.semaphore_wait(barrier, jnp.where((me > 0) & (me < n - 1), 2 + extra, 1 + extra))
    return me


class LineSum:
    def __init__(self, n, me, middle, part, out, held, sems):
        self.n, self.me, self.middle, self.part, self.out = n, me, middle, part, out
        self.from_left, self.from_right, self.to_right, self.to_left = held
        self.rs_send, self.rs_recv, self.ag_send, self.ag_recv = sems
        self.stages = 2 * n - 1

    def reduce_copy(self, src, landing, side, chunk, block, target):
        return pltpu.make_async_remote_copy(
            src_ref=src,
            dst_ref=landing.at[chunk, block],
            send_sem=self.rs_send.at[side, chunk, block],
            recv_sem=self.rs_recv.at[side, chunk, block],
            device_id={"tensor": target},
            device_id_type=MESH,
        )

    def gather_copy(self, side, chunk, block, target):
        return pltpu.make_async_remote_copy(
            src_ref=self.out.at[chunk, block],
            dst_ref=self.out.at[chunk, block],
            send_sem=self.ag_send.at[side, chunk, block],
            recv_sem=self.ag_recv.at[chunk, block],
            device_id={"tensor": target},
            device_id_type=MESH,
        )

    def put(self, chunk, rows):
        self.part[chunk] = rows.astype(bf16).reshape(self.part.shape[1:])

    def rows(self, chunk):
        whole = self.out[chunk]
        return whole.reshape(-1, whole.shape[-1])

    def stage(self, chunk, stage):
        n = self.n
        if stage == 0:
            self.first_sends(chunk)
        elif stage <= n - 2:
            self.hop(chunk, stage)
        elif stage == n - 1:
            self.own_rows(chunk)
        else:
            self.forward(chunk, stage - n + 1)

    def first_sends(self, chunk):
        n, part = self.n, self.part

        @pl.when(self.me == 0)
        def _():
            for block in range(n - 1, 0, -1):
                self.reduce_copy(
                    part.at[chunk, block], self.from_left, 0, chunk, block, 1
                ).start()

        @pl.when(self.me == n - 1)
        def _():
            for block in range(n - 1):
                self.reduce_copy(
                    part.at[chunk, block], self.from_right, 1, chunk, block, n - 2
                ).start()

    def hop(self, chunk, step):
        n, part = self.n, self.part

        @pl.when(self.me == step)
        def _():
            landing, sent = self.from_left, self.to_right
            for block in range(n - 1, step, -1):
                self.reduce_copy(
                    part.at[chunk, block], landing, 0, chunk, block, step
                ).wait_recv()
                sent[chunk, block] = (
                    landing[chunk, block].astype(f32) + part[chunk, block].astype(f32)
                ).astype(bf16)
                self.reduce_copy(
                    sent.at[chunk, block], landing, 0, chunk, block, step + 1
                ).start()

        @pl.when(self.me == n - 1 - step)
        def _():
            landing, sent = self.from_right, self.to_left
            mine = n - 1 - step
            for block in range(mine):
                self.reduce_copy(
                    part.at[chunk, block], landing, 1, chunk, block, mine
                ).wait_recv()
                sent[chunk, block] = (
                    landing[chunk, block].astype(f32) + part[chunk, block].astype(f32)
                ).astype(bf16)
                self.reduce_copy(
                    sent.at[chunk, block], landing, 1, chunk, block, mine - 1
                ).start()

    def own_rows(self, chunk):
        n, me, part = self.n, self.me, self.part

        @pl.when(me > 0)
        def _():
            self.reduce_copy(part.at[chunk, me], self.from_left, 0, chunk, me, me).wait_recv()

        @pl.when(me < n - 1)
        def _():
            self.reduce_copy(part.at[chunk, me], self.from_right, 1, chunk, me, me).wait_recv()

        total = part[chunk, me].astype(f32)
        total = total + jnp.where(me > 0, self.from_left[chunk, me].astype(f32), 0.0)
        total = total + jnp.where(me < n - 1, self.from_right[chunk, me].astype(f32), 0.0)
        self.out[chunk, me] = self.middle(chunk, me, total).astype(bf16)

        @pl.when(me < n - 1)
        def _():
            self.gather_copy(0, chunk, me, me + 1).start()

        @pl.when(me > 0)
        def _():
            self.gather_copy(1, chunk, me, me - 1).start()

    def forward(self, chunk, step):
        n, me = self.n, self.me
        left_block = me - step

        @pl.when(left_block >= 0)
        def _():
            self.gather_copy(0, chunk, left_block, me).wait_recv()

            @pl.when(me < n - 1)
            def _():
                self.gather_copy(0, chunk, left_block, me + 1).start()

        right_block = me + step

        @pl.when(right_block < n)
        def _():
            self.gather_copy(1, chunk, right_block, me).wait_recv()

            @pl.when(me > 0)
            def _():
                self.gather_copy(1, chunk, right_block, me - 1).start()

    def finish(self):
        n, me, part = self.n, self.me, self.part
        for chunk in range(part.shape[0]):
            for block in range(n):

                @pl.when((me < n - 1) & (block > me))
                def _():
                    self.reduce_copy(
                        part.at[chunk, block], self.from_left, 0, chunk, block, me
                    ).wait_send()

                @pl.when((me > 0) & (block < me))
                def _():
                    self.reduce_copy(
                        part.at[chunk, block], self.from_right, 1, chunk, block, me
                    ).wait_send()

                @pl.when((me < n - 1) & (block <= me))
                def _():
                    self.gather_copy(0, chunk, block, me).wait_send()

                @pl.when((me > 0) & (block >= me))
                def _():
                    self.gather_copy(1, chunk, block, me).wait_send()


def line_scratch(chunks, n, block, width):
    return [pltpu.VMEM((chunks, n, block, width), bf16)] * 5 + [
        pltpu.SemaphoreType.DMA((2, chunks, n)),
        pltpu.SemaphoreType.DMA((2, chunks, n)),
        pltpu.SemaphoreType.DMA((2, chunks, n)),
        pltpu.SemaphoreType.DMA((chunks, n)),
    ]


def make_line(n, me, middle, out, scratch):
    return LineSum(n, me, middle, scratch[0], out, scratch[1:5], scratch[5:9])


def run_two(order, first, second, produce, between, finished, extra):
    lag = first.stages - 1
    last = len(order) - 1
    for slot in range(2 * lag + last + 1):
        if slot <= last:
            produce(order[slot])
        for place, chunk in enumerate(order):
            stage = slot - lag - place
            if 1 <= stage <= lag:
                second.stage(chunk, stage)
            if stage == lag:
                finished(chunk)
        if slot > lag + last:
            extra(slot - lag - last)
        for place, chunk in enumerate(order):
            stage = slot - place
            if 0 <= stage <= lag:
                first.stage(chunk, stage)
        if 0 <= slot - lag <= last:
            chunk = order[slot - lag]
            between(chunk)
            second.stage(chunk, 0)


def score_columns(head, chunk, q_ref, kv_ref, docs, keys_docs):
    lanes = slice(head * HD, (head + 1) * HD)
    width = CMEM + MEM + (chunk + 1) * ROWS
    query = q_ref[chunk * ROWS : (chunk + 1) * ROWS, lanes]
    scores = dot_nt(kv_ref[:width, lanes], query) * HD ** (-0.5)
    own = docs[:, chunk * ROWS : (chunk + 1) * ROWS]
    same = keys_docs[: MEM + chunk * ROWS, :] == own
    tail_docs = keys_docs[MEM + chunk * ROWS : MEM + (chunk + 1) * ROWS, :]
    key_place = lax.broadcasted_iota(jnp.int32, (ROWS, ROWS), 0)
    query_place = lax.broadcasted_iota(jnp.int32, (ROWS, ROWS), 1)
    tail_same = (tail_docs == own) & (key_place <= query_place)
    middle_end = CMEM + MEM + chunk * ROWS
    return jnp.concatenate(
        [
            scores[:CMEM],
            jnp.where(same, scores[CMEM:middle_end], masked_value),
            jnp.where(tail_same, scores[middle_end:], masked_value),
        ],
        axis=0,
    )


def forward_kernel(n, ship, *refs):
    (c_ref, m_ref, x_ref, wq, wkv, wo, wup, wdown, gains, docs, key_docs) = refs[:11]
    (normed, q_ref, kv_ref, log_sum, attended, residual, two, hidden, active) = refs[11:20]
    out = refs[20]
    rest = refs[21:]
    if ship:
        shipped, rest = rest[0], rest[1:]
    keys_docs, values_t = rest[:2]
    first_scratch, second_scratch = rest[2:11], rest[11:20]
    if ship:
        ship_send, ship_recv = rest[20:22]
    me = greet(n, ship)
    section = lax.axis_index("section")
    heads = wq.shape[1] // HD
    local = wq.shape[1]

    keys_docs[...] = jnp.broadcast_to(key_docs[...], keys_docs.shape)
    gain_a = gains[0:1, :]
    gain_f = gains[1:2, :]

    def project_block(source, place):
        def body(step, carry):
            rows = pl.ds(pl.multiple_of(step * 256, 256), 256)
            at = pl.ds(pl.multiple_of(place * SEG + step * 256, 256), 256)
            wide = source[rows, :].astype(f32)
            block = (wide * inverse_rms(wide) * gain_a).astype(bf16)
            normed[at, :] = block
            both = dot_nn(block, wkv[...]).astype(bf16)
            kv_ref[at, :] = both
            if place == 2:
                q_ref[rows, :] = dot_nn(block, wq[...]).astype(bf16)
            return carry

        lax.fori_loop(0, SEG // 256, body, 0)

    project_block(c_ref, 0)
    project_block(m_ref, 1)
    x_rows = x_ref.reshape(SEG, x_ref.shape[-1])
    project_block(x_rows, 2)
    for head in range(heads):
        lanes = slice(local + head * HD, local + (head + 1) * HD)
        values_t[head] = kv_ref[:, lanes].astype(f32).T.astype(bf16)

    def attention_middle(chunk, me, total):
        rows = x_ref[chunk, me].astype(f32) + total
        residual[chunk] = rows
        return rows * inverse_rms(rows) * gain_f

    def output_middle(chunk, me, total):
        return residual[chunk] + total

    first = make_line(n, me, attention_middle, two, first_scratch)
    second = make_line(n, me, output_middle, out, second_scratch)

    def attend(chunk):
        rows = slice(chunk * ROWS, (chunk + 1) * ROWS)
        for head in range(heads):
            lanes = slice(head * HD, (head + 1) * HD)
            scores = score_columns(head, chunk, q_ref, kv_ref, docs, keys_docs)
            top = jnp.max(scores, axis=0, keepdims=True)
            powers = jnp.exp(scores - top)
            total = jnp.sum(powers, axis=0, keepdims=True)
            log_sum[head : head + 1, rows] = top + jnp.log(total)
            weights = (powers * (1.0 / total)).astype(bf16)
            mixed = dot_nn(values_t[head, :, : weights.shape[0]], weights)
            attended[rows, lanes] = mixed.T.astype(bf16)
        first.put(chunk, dot_nn(attended[rows, :], wo[...]))

    def feed(chunk):
        rows = slice(chunk * ROWS, (chunk + 1) * ROWS)
        before = dot_nn(first.rows(chunk), wup[...])
        hidden[rows, :] = before
        after = gelu(before).astype(bf16)
        active[rows, :] = after
        second.put(chunk, dot_nn(after, wdown[...]))

    def ship_copy(chunk):
        return pltpu.make_async_remote_copy(
            src_ref=out.at[chunk],
            dst_ref=shipped.at[chunk],
            send_sem=ship_send.at[chunk],
            recv_sem=ship_recv.at[chunk],
            device_id={"section": 1 - section},
            device_id_type=MESH,
        )

    def finished(chunk):
        if ship:

            @pl.when(section == 0)
            def _():
                ship_copy(chunk).start()

    run_two(list(range(CHUNKS)), first, second, attend, feed, finished, lambda step: None)
    first.finish()
    second.finish()
    if ship:
        for chunk in range(CHUNKS):

            @pl.when(section == 0)
            def _():
                ship_copy(chunk).wait_send()

            @pl.when(section == 1)
            def _():
                ship_copy(chunk).wait_recv()


def vmem_specs(count):
    return [pl.BlockSpec(memory_space=pltpu.VMEM)] * count


def forward_layer(collective, n, ship, c_rows, m_rows, x_rows, weights, gains, docs, key_docs):
    wq, wkv, wo, wup, wdown = weights
    width = x_rows.shape[1]
    local = wq.shape[1]
    hidden = wup.shape[1]
    block = ROWS // n
    shape = jax.ShapeDtypeStruct
    rows = shape((CHUNKS, n, block, width), bf16)
    outs = [
        shape((CMEM + MEM + SEG, width), bf16),
        shape((SEG, local), bf16),
        shape((CMEM + MEM + SEG, 2 * local), bf16),
        shape((8, SEG), f32),
        shape((SEG, local), bf16),
        shape((CHUNKS, block, width), f32),
        rows,
        shape((SEG, hidden), f32),
        shape((SEG, hidden), bf16),
        rows,
    ] + ([rows] if ship else [])
    result = pl.pallas_call(
        functools.partial(forward_kernel, n, ship),
        name="forward_ship" if ship else "forward_last",
        out_shape=outs,
        in_specs=vmem_specs(11),
        out_specs=vmem_specs(len(outs)),
        scratch_shapes=[
            pltpu.VMEM((MEM + SEG, HD), jnp.int32),
            pltpu.VMEM((local // HD, HD, CMEM + MEM + SEG), bf16),
        ]
        + line_scratch(CHUNKS, n, block, width)
        + line_scratch(CHUNKS, n, block, width)
        + ([pltpu.SemaphoreType.DMA((CHUNKS,))] * 2 if ship else []),
        compiler_params=pltpu.CompilerParams(
            collective_id=collective, has_side_effects=True, vmem_limit_bytes=60000 * 1024
        ),
    )(c_rows, m_rows, x_rows.reshape(CHUNKS, n, block, width), wq, wkv, wo, wup, wdown, gains,
      docs, key_docs)
    return result


def backward_kernel(n, *refs):
    (g_ref, x_ref, residual, hidden, fresh, wq, wkv, wo, wup, wdown, gains, q_ref, kv_ref,
     log_sum, docs, key_docs) = refs[:16]
    d_hidden, d_branch, dq_ref, dkv_ref, dx_ref, d_fresh = refs[16:22]
    d_residual, keys_docs, keys_t, sums = refs[22:26]
    first_scratch, second_scratch, fresh_scratch = refs[26:35], refs[35:44], refs[44:53]
    me = greet(n, False)
    late = lax.axis_index("section") == 1
    local = wq.shape[1]
    heads = local // HD
    gain_a = gains[0:1, :]
    gain_f = gains[1:2, :]
    scale = HD ** (-0.5)

    keys_docs[...] = jnp.broadcast_to(key_docs[...], keys_docs.shape)
    for head in range(heads):
        lanes = slice(head * HD, (head + 1) * HD)
        keys_t[head] = kv_ref[:, lanes].astype(f32).T.astype(bf16)

    def branch_middle(chunk, me, total):
        rows = g_ref[chunk, me].astype(f32) + rms_pull(total, residual[chunk], gain_f)
        d_residual[chunk] = rows
        return rows

    def input_middle(chunk, me, total):
        return d_residual[chunk] + rms_pull(total, x_ref[chunk, me].astype(f32), gain_a)

    def fresh_middle(chunk, me, total):
        return rms_pull(total, fresh[chunk, me].astype(f32), gain_a)

    first = make_line(n, me, branch_middle, d_branch, first_scratch)
    second = make_line(n, me, input_middle, dx_ref, second_scratch)
    third = make_line(n, me, fresh_middle, d_fresh, fresh_scratch)

    def produce(chunk):
        rows = slice(chunk * ROWS, (chunk + 1) * ROWS)
        grad = g_ref[chunk]
        d_active = dot_nt(grad.reshape(ROWS, grad.shape[-1]), wdown[...])
        block = (gelu_slope(hidden[rows, :]) * d_active).astype(bf16)
        d_hidden[rows, :] = block
        first.put(chunk, dot_nt(block, wup[...]))

    def attend_back(chunk):
        rows = slice(chunk * ROWS, (chunk + 1) * ROWS)
        d_attended = dot_nt(first.rows(chunk), wo[...]).astype(bf16)
        fresh_sum = chunk == CHUNKS - 1
        for head in range(heads):
            lanes = slice(head * HD, (head + 1) * HD)
            value_lanes = slice(local + head * HD, local + (head + 1) * HD)
            scores = score_columns(head, chunk, q_ref, kv_ref, docs, keys_docs)
            size = scores.shape[0]
            probs = jnp.exp(scores - log_sum[head : head + 1, rows])
            d_mixed = d_attended[:, lanes]
            d_values = dot_nn(probs.astype(bf16), d_mixed)
            d_probs = dot_nt(kv_ref[:size, value_lanes], d_mixed)
            inner = jnp.sum(d_probs * probs, axis=0, keepdims=True)
            d_scores = (probs * (d_probs - inner)).astype(bf16)
            d_keys = dot_nn(d_scores, q_ref[rows, lanes])
            d_queries = dot_nn(keys_t[head, :, :size], d_scores) * scale
            dq_ref[rows, lanes] = d_queries.T.astype(bf16)
            if fresh_sum:
                sums[:size, lanes] = d_keys
                sums[:size, value_lanes] = d_values
            else:
                sums[:size, lanes] += d_keys
                sums[:size, value_lanes] += d_values
        own = slice(CMEM + MEM + chunk * ROWS, CMEM + MEM + (chunk + 1) * ROWS)
        close_rows(own)
        second.put(
            chunk, dot_nt(dq_ref[rows, :], wq[...]) + dot_nt(dkv_ref[own, :], wkv[...])
        )
        if chunk == 0:
            close_rows(slice(0, CMEM + MEM))

            @pl.when(late)
            def _():
                count = third.part.shape[1] * third.part.shape[2]
                third.put(0, dot_nt(dkv_ref[FRESH_START : FRESH_START + count, :], wkv[...]))
                third.stage(0, 0)

    def close_rows(rows):
        dkv_ref[rows, :local] = (sums[rows, :local] * scale).astype(bf16)
        dkv_ref[rows, local:] = sums[rows, local:].astype(bf16)

    def extra(step):
        if step < third.stages:

            @pl.when(late)
            def _():
                third.stage(0, step)

    run_two(
        list(range(CHUNKS - 1, -1, -1)), first, second, produce, attend_back,
        lambda chunk: None, extra,
    )
    first.finish()
    second.finish()

    @pl.when(late)
    def _():
        third.finish()


def fresh_block(n):
    return -(-(CMEM - FRESH_START) // (16 * n)) * 16


def backward_layer(collective, n, grad, x_rows, residual, hidden, fresh, weights, gains, q, kv,
                   log_sum, docs, key_docs):
    wq, wkv, wo, wup, wdown = weights
    width = wo.shape[1]
    local = wq.shape[1]
    block = ROWS // n
    shape = jax.ShapeDtypeStruct
    rows = shape((CHUNKS, n, block, width), bf16)
    outs = [
        shape((SEG, wup.shape[1]), bf16),
        rows,
        shape((SEG, local), bf16),
        shape((CMEM + MEM + SEG, 2 * local), bf16),
        rows,
        shape((1, n, fresh_block(n), width), bf16),
    ]
    return pl.pallas_call(
        functools.partial(backward_kernel, n),
        name="backward",
        out_shape=outs,
        in_specs=vmem_specs(16),
        out_specs=vmem_specs(len(outs)),
        scratch_shapes=[
            pltpu.VMEM((CHUNKS, block, width), f32),
            pltpu.VMEM((MEM + SEG, HD), jnp.int32),
            pltpu.VMEM((local // HD, HD, CMEM + MEM + SEG), bf16),
            pltpu.VMEM((CMEM + MEM + SEG, 2 * local), f32),
        ]
        + line_scratch(CHUNKS, n, block, width)
        + line_scratch(CHUNKS, n, block, width)
        + line_scratch(1, n, fresh_block(n), width),
        compiler_params=pltpu.CompilerParams(
            collective_id=collective, has_side_effects=True, vmem_limit_bytes=60000 * 1024
        ),
    )(grad.reshape(rows.shape), x_rows.reshape(rows.shape), residual, hidden, fresh,
      wq, wkv, wo, wup, wdown, gains, q, kv, log_sum, docs, key_docs)


def gather_kernel(n, x_ref, out, send, recv):
    me = greet(n, False)

    def copy(side, block, target):
        return pltpu.make_async_remote_copy(
            src_ref=out.at[block],
            dst_ref=out.at[block],
            send_sem=send.at[side, block],
            recv_sem=recv.at[block],
            device_id={"tensor": target},
            device_id_type=MESH,
        )

    out[me] = x_ref[...]

    @pl.when(me < n - 1)
    def _():
        copy(0, me, me + 1).start()

    @pl.when(me > 0)
    def _():
        copy(1, me, me - 1).start()

    for step in range(1, n):
        left_block = me - step

        @pl.when(left_block >= 0)
        def _():
            copy(0, left_block, me).wait_recv()

            @pl.when(me < n - 1)
            def _():
                copy(0, left_block, me + 1).start()

        right_block = me + step

        @pl.when(right_block < n)
        def _():
            copy(1, right_block, me).wait_recv()

            @pl.when(me > 0)
            def _():
                copy(1, right_block, me - 1).start()

    for block in range(n):

        @pl.when((me < n - 1) & (block <= me))
        def _():
            copy(0, block, me).wait_send()

        @pl.when((me > 0) & (block >= me))
        def _():
            copy(1, block, me).wait_send()


def gather_line(name, collective, n, x):
    return pl.pallas_call(
        functools.partial(gather_kernel, n),
        name=name,
        out_shape=jax.ShapeDtypeStruct((n,) + x.shape, x.dtype),
        in_specs=vmem_specs(1),
        out_specs=pl.BlockSpec(memory_space=pltpu.VMEM),
        scratch_shapes=[pltpu.SemaphoreType.DMA((2, n)), pltpu.SemaphoreType.DMA((n,))],
        compiler_params=pltpu.CompilerParams(collective_id=collective, has_side_effects=True),
    )(x)


def project(rows, weight):
    return jnp.dot(rows, weight, preferred_element_type=f32).astype(bf16)


def shards(
    block_input,
    doc_ids,
    memory,
    compressed,
    gain_attn,
    w_query,
    w_key,
    w_value,
    w_out,
    gain_ffn,
    w_up,
    w_down,
    w_compress,
    cotangent,
):
    section = lax.axis_index("section")
    first = section == 0
    n = lax.axis_size("tensor")
    groups = lax.axis_size("dp")
    tensor_index = lax.axis_index("tensor")
    dp_index = lax.axis_index("dp")
    width = block_input.shape[2]
    local = w_query.shape[2]
    both = [(0, 1), (1, 0)]
    forth, back = [(0, 1)], [(1, 0)]

    core = dp_index % 2
    row = dp_index // 2
    rows_y = groups // 2
    core_pairs = [(i, i ^ 1) for i in range(groups)]

    def row_pairs(step):
        return [(i, (i + 2 * step) % groups) for i in range(groups)]

    def swap_weight(weight):
        rows = weight.shape[0] // groups
        piece = lax.dynamic_slice_in_dim(weight, dp_index * rows, rows, 0)
        piece = lax.ppermute(piece, "section", both)
        partner = lax.ppermute(piece, "dp", core_pairs)
        pair = jnp.where(
            core == 0,
            jnp.concatenate([piece, partner]),
            jnp.concatenate([partner, piece]),
        )
        whole = jnp.zeros(weight.shape, weight.dtype)
        whole = lax.dynamic_update_slice_in_dim(whole, pair, row * 2 * rows, 0)
        for step in range(1, rows_y):
            other = lax.ppermute(pair, "dp", row_pairs(step))
            place = (row - step) % rows_y
            whole = lax.dynamic_update_slice_in_dim(whole, other, place * 2 * rows, 0)
        return whole

    def scatter_rows(array):
        blocks = array.reshape(rows_y, 2, width // groups, array.shape[1])
        kept = lax.dynamic_index_in_dim(blocks, core, 1, keepdims=False)
        sent = lax.dynamic_index_in_dim(blocks, 1 - core, 1, keepdims=False)
        kept = (kept.astype(f32) + lax.ppermute(sent, "dp", core_pairs).astype(f32)).astype(bf16)
        total = lax.dynamic_index_in_dim(kept, row, 0, keepdims=False).astype(f32)
        for step in range(1, rows_y):
            sent = lax.dynamic_index_in_dim(kept, (row + step) % rows_y, 0, keepdims=False)
            total = total + lax.ppermute(sent, "dp", row_pairs(step)).astype(f32)
        return total

    def by_layer(own, other):
        return [jnp.where(first, own, other), jnp.where(first, other, own)]

    gains = jnp.stack([gain_attn[0], gain_ffn[0]])
    gains_other = lax.ppermute(gains, "section", both)
    gains_by_layer = by_layer(gains, gains_other)

    own_weights = (
        w_query[0], jnp.concatenate([w_key[0], w_value[0]], axis=1), w_out[0], w_up[0], w_down[0],
    )
    weight_layers = list(
        zip(*[by_layer(weight, swap_weight(weight)) for weight in own_weights])
    )

    history = doc_ids[0]
    memory_docs = lax.dynamic_slice_in_dim(history, section * SEG, MEM, 0)
    token_docs = lax.dynamic_slice_in_dim(history, MEM + section * SEG, SEG, 0)
    docs = token_docs[None]
    key_docs = jnp.concatenate([memory_docs, token_docs])[:, None]
    early, later = block_input[0, :SEG], block_input[0, SEG:]
    grad_now = lax.dynamic_slice_in_dim(cotangent[0], section * SEG, SEG, 0)

    padded = jnp.concatenate([jnp.zeros((PAD, width), bf16), memory[0, 0]]).reshape(
        COMP_ROWS, RATE * width
    )
    fresh_piece = project(padded, w_compress[0].reshape(RATE * width, local))
    fresh = gather_line("gather_fresh", 8, n, fresh_piece)
    fresh = fresh.transpose(1, 0, 2).reshape(COMP_ROWS, width)
    late_rows = jnp.concatenate([compressed[0, 0, COMP_ROWS:], fresh])
    sent_rows = lax.ppermute(jnp.where(first, late_rows, compressed[0, 0]), "section", both)
    sent_memory = lax.ppermute(memory[0, 0], "section", back)
    c_rows = [
        jnp.where(first, compressed[0, 0], sent_rows), jnp.where(first, sent_rows, late_rows),
    ]

    saved = []
    outputs = []
    tokens = jnp.where(first, early, later)
    m_rows = jnp.where(first, memory[0, 0], early)
    for layer in range(2):
        result = forward_layer(
            1 + layer, n, layer == 0, c_rows[layer], m_rows, tokens, weight_layers[layer],
            gains_by_layer[layer], docs, key_docs,
        )
        normed, queries, kv, log_total, attended, residual, two, hidden, active, out = result[:10]
        saved.append((tokens, m_rows, normed, queries, kv, log_total, attended, residual,
                      two.reshape(SEG, width), hidden, active))
        tokens = out.reshape(SEG, width)
        outputs.append(tokens)
        if layer == 0:
            m_rows = jnp.where(first, sent_memory, result[10].reshape(SEG, width))

    grads = [None, None]
    input_grads = [None, None]
    fresh_grads = [None, None]
    for layer in (1, 0):
        (tokens, m_rows, normed, queries, kv, log_total, attended, residual, two, hidden,
         active) = saved[layer]
        block = fresh_block(n)
        fresh_rows = jnp.concatenate(
            [c_rows[layer][FRESH_START:], m_rows[: n * block - (CMEM - FRESH_START)]]
        ).reshape(1, n, block, width)
        d_hidden, d_branch, dq, dkv, dx, d_fresh = backward_layer(
            4, n, grad_now, tokens, residual, hidden, fresh_rows, weight_layers[layer],
            gains_by_layer[layer], queries, kv, log_total, docs, key_docs,
        )
        d_branch = d_branch.reshape(SEG, width)
        grad = jnp.concatenate(
            [
                dot_tn(normed[CMEM + MEM :], dq).astype(bf16),
                dot_tn(normed, dkv).astype(bf16),
                dot_tn(d_branch, attended).astype(bf16),
                dot_tn(two, d_hidden).astype(bf16),
                dot_tn(grad_now, active).astype(bf16),
            ],
            axis=1,
        )
        grad_now = dx.reshape(SEG, width)
        input_grads[layer] = grad_now
        share = scatter_rows(grad)
        grads[layer] = (
            share, lax.ppermute(share.astype(bf16), "section", forth if layer == 1 else back)
        )
        skip = OLD_ROWS - FRESH_START
        d_fresh = d_fresh.reshape(n * block, width)[skip : skip + COMP_ROWS]
        fresh_grads[layer] = lax.dynamic_slice_in_dim(d_fresh, tensor_index * local, local, 1)

    d_fresh = jnp.where(
        first, lax.ppermute(fresh_grads[0], "section", back), fresh_grads[1]
    )
    grad_compress = dot_tn(padded, d_fresh).astype(bf16)
    compress_share = scatter_rows(
        jnp.concatenate(
            [grad_compress[place * width : (place + 1) * width] for place in range(RATE)], axis=1
        )
    )
    share = jnp.where(first, grads[0][0], grads[1][0]) + jnp.where(
        first, grads[0][1], grads[1][1]
    ).astype(f32)
    rows = width // groups
    up_local = w_up.shape[2]
    qkv_share = share[:, : 3 * local]
    out_share = share[:, 3 * local : 4 * local]
    up_share = share[:, 4 * local : 4 * local + up_local]
    down_share = share[:, 4 * local + up_local :]
    compress_share = compress_share.reshape(rows, RATE, local)

    def my_rows(weight):
        return lax.dynamic_slice_in_dim(weight, dp_index * rows, rows, 0).astype(f32)

    my_qkv = jnp.concatenate([my_rows(w_query[0]), my_rows(w_key[0]), my_rows(w_value[0])], axis=1)
    sums = jnp.stack(
        [jnp.sum(my_qkv * qkv_share, axis=1), jnp.sum(my_rows(w_up[0]) * up_share, axis=1)]
    )
    my_gains = lax.dynamic_slice_in_dim(gains, dp_index * rows, rows, 1)
    sums = gather_line("gather_sums", 9, n, jnp.pad(sums, ((0, 6), (0, 0))))
    gain_grads = jnp.sum(sums, axis=0)[:2] / my_gains

    return (
        assemble(outputs, first),
        assemble(input_grads, first),
        gain_grads[:1],
        qkv_share[None, :, :local],
        qkv_share[None, :, local : 2 * local],
        qkv_share[None, :, 2 * local :],
        out_share.T[None],
        gain_grads[1:],
        up_share[None],
        down_share.T[None],
        compress_share.transpose(1, 0, 2)[None],
    )


def assemble(pieces, first):
    own = jnp.where(first, pieces[0], pieces[1])
    other = lax.ppermute(
        jnp.where(first, pieces[1], pieces[0]), "section", [(0, 1), (1, 0)]
    )
    return jnp.concatenate(
        [jnp.where(first, own, other), jnp.where(first, other, own)]
    )[None, None]


def solution(mesh):
    return jax.shard_map(
        shards,
        mesh=mesh,
        in_specs=(
            P("dp", None, None),
            P("dp", None),
            P("section", "dp", None, None),
            P("section", "dp", None, None),
            P("section", None),
            P("section", None, "tensor"),
            P("section", None, "tensor"),
            P("section", None, "tensor"),
            P("section", "tensor", None),
            P("section", None),
            P("section", None, "tensor"),
            P("section", "tensor", None),
            P("section", None, None, "tensor"),
            P("dp", None, None),
        ),
        out_specs=(
            P("section", "dp", None, None),
            P("section", "dp", None, None),
            P("section", "dp"),
            P("section", "dp", "tensor"),
            P("section", "dp", "tensor"),
            P("section", "dp", "tensor"),
            P("section", "tensor", "dp"),
            P("section", "dp"),
            P("section", "dp", "tensor"),
            P("section", "tensor", "dp"),
            P("section", None, "dp", "tensor"),
        ),
        check_vma=False,
    )
```

time: 1410 us -> 692 us (0.49)
  waiting for transfers between devices: 847 us -> 115 us
  Pallas kernels: 0 us -> 349 us
  matrix products: 191 us -> 31.4 us
  other arithmetic: 153 us -> 66.6 us
  local copies, waits for them, and re-layouts: 155 us -> 70.1 us
  starting transfers between devices: 13.5 us -> 49.2 us
  blocking collectives: 26.3 us -> 0 us
  between operations: 17.1 us -> 1.88 us
    psum x11 -> x0, waiting for transfers between devices: 634 us -> none  [the longest x4 209 us: attention_branch(): lax.psum(partial_value.astype(jnp.bfloat16), 'tensor').astype(jnp.float32)]
    pallas_call x0 -> x6, Pallas kernels: none -> 349 us  [the longest x2 168 us: forward_layer(): pl.pallas_call(functools.partial(forward_kernel, n, ship), name='forward_...]
    dot_general x94 -> x12, matrix products: 191 us -> 31.4 us  [the longest x11 28.9 us: dot_tn(): lax.dot_general(a, b, (((0,), (0,)), ((), ())), preferred_element_type=f32)]
    unnamed x13 -> x0, waiting for transfers between devices: 136 us -> none
    reduce_sum x26 -> x2, other arithmetic: 58.9 us -> 2.1 us  [the longest x1 1.34 us: shards(): jnp.sum(my_qkv * qkv_share, axis=1)]
    unnamed x423 -> x99, local copies, waits for them, and re-layouts: 52.7 us -> 13.5 us
    ppermute x4 -> x29, waiting for transfers between devices: 76.7 us -> 115 us  [the longest x3 43.1 us: scatter_rows(): total = total + lax.ppermute(sent, 'dp', row_pairs(step)).astype(f32)]
    ppermute x4 -> x29, starting transfers between devices: 11.8 us -> 49.2 us  [the longest x2 20.9 us: assemble(): lax.ppermute(jnp.where(first, pieces[1], pieces[0]), 'section', [(0, 1),...]
  transfers between devices with their start and end apart: 16 -> 29, of which waited for: 16 -> 8; matrix products, arithmetic and copies ran while one was open for 9% -> 18% of each run, Pallas kernels for 0% -> 27%
where the time goes in v1:
time: 692 us; the launch traced here: 684 us
  Pallas kernels  349 us (50%)
  waiting for transfers between devices  115 us (17%)
  local copies, waits for them, and re-layouts  70.1 us (10%)
  other arithmetic  66.6 us (10%)
  starting transfers between devices  49.2 us (7%)
  matrix products  31.4 us (5%)
    pallas_call x2, Pallas kernels, forward_layer(): pl.pallas_call(functools.partial(forward_kernel, n, ship), name='forward_...  168 us
    pallas_call x2, Pallas kernels, backward_layer(): pl.pallas_call(functools.partial(backward_kernel, n), name='backward', ou...  156 us
    ppermute x3, waiting for transfers between devices, scatter_rows(): total = total + lax.ppermute(sent, 'dp', row_pairs(step)).astype(f32)  43.1 us
    ppermute x1, waiting for transfers between devices, shards(): lax.ppermute(jnp.where(first, late_rows, compressed[0, 0]), 'section', both)  34.8 us
    dot_general x11, matrix products, dot_tn(): lax.dot_general(a, b, (((0,), (0,)), ((), ())), preferred_element_type=f32)  28.9 us
    pallas_call x2, Pallas kernels, gather_line(): pl.pallas_call(functools.partial(gather_kernel, n), name=name, out_shape=...  25.7 us
    ppermute x2, waiting for transfers between devices, shards(): lax.ppermute(share.astype(bf16), 'section', forth if layer == 1 else back)  24.1 us
    ppermute x2, starting transfers between devices, assemble(): lax.ppermute(jnp.where(first, pieces[1], pieces[0]), 'section', [(0, 1),...  20.9 us
  transfers between devices with their start and end apart: 29, of which 8 were waited for; matrix products, arithmetic and copies ran while one was open for 18% of the time, Pallas kernels for 27%

profile of v1, /device:TPU:0, one launch (start us, length us, event | category | flops | bytes accessed | tf_op | source)
XLA Modules:
  0.0 683.7 jit_solution(13157506059116857473)
XLA Ops:
  2.1 3.0 collective-permute-start.16
  5.1 1.6 dynamic-slice_bitcast_fusion.10
  6.7 1.6 dynamic-slice_bitcast_fusion.9
  8.2 2.0 collective-permute-start.7
  10.3 1.7 fusion.15
  12.0 1.9 dynamic-slice_bitcast_fusion.4
  13.8 2.0 collective-permute-start.13
  16.9 2.7 slice_select_fusion
  19.5 2.3 bitcast_select_fusion.9.refs_1_
  21.8 2.5 concatenate.69
  24.3 1.6 reshape.115
  25.9 2.5 convolution_convert_fusion.7.x_ref
  28.4 15.4 %gather_fresh.1 = bf16[4,171,256]{2,1,0:T(8,128)(2,1)} custom-call(bf16[171,256]{1,0:T(8,128)(2,1)} %convolution_convert_fusion.7.x_ref), custom_call_target="tpu_custom_call" | custom-call | tf_op jit(solution)/shard_map/gather_fresh/pallas_call | solution.py:663
  45.2 2.8 bitcast_select_fusion.11
  54.2 1.6 collective-permute-start.9
  61.7 1.7 collective-permute-done.9
  63.4 1.7 collective-permute-start
  65.2 2.7 collective-permute-done.3
  70.8 1.7 constant_dynamic-update-slice_fusion.1
  73.9 1.6 collective-permute-start.12
  76.6 34.8 %collective-permute-done = bf16[512,1024]{1,0:T(8,128)(2,1)S(1)} collective-permute-done((bf16[512,1024]{1,0:T(8,128)(2,1)S(1)}, bf16[512,1024]{1,0:T(8,128)(2,1)S(1)}, u32[]{:S(2)}, u32[]{:S(2)}) %collective-permute-start) | collective-permute-done | bytes 1048608 | tf_op jit(solution)/shard_map/ppermute | solution.py:771
  114.1 1.8 broadcast_select_fusion
  116.7 8.8 %collective-permute-done.12 = bf16[512,1024]{1,0:T(8,128)(2,1)S(1)} collective-permute-done((bf16[512,1024]{1,0:T(8,128)(2,1)S(1)}, bf16[512,1024]{1,0:T(8,128)(2,1)S(1)}, u32[]{:S(2)}, u32[]{:S(2)}) %collective-permute-start.12) | collective-permute-done | bytes 1048608 | tf_op jit(solution)/shard_map/ppermute | solution.py:726
  127.2 2.4 bitcast_select_fusion
  129.6 2.5 bitcast_select_fusion.2
  132.1 87.3 %forward_ship.1 = (bf16[1536,1024]{1,0:T(8,128)(2,1)}, bf16[512,256]{1,0:T(8,128)(2,1)}, bf16[1536,512]{1,0:T(8,128)(2,1)}, f32[8,512]{1,0:T(8,128)}, bf16[512,2...) custom-call(bf16[512,1024]{1,0:T(8,128)(2,1)} %copy-done.14, ...), custom_call_target="tpu_custom_call" | custom-call | tf_op jit(solution)/shard_map/forward_ship/pallas_call | solution.py:441
  219.5 1.7 bitcast_select_fusion.8.refs_1_
  222.3 80.2 %forward_last.1 = (bf16[1536,1024]{1,0:T(8,128)(2,1)}, bf16[512,256]{1,0:T(8,128)(2,1)}, bf16[1536,512]{1,0:T(8,128)(2,1)}, f32[8,512]{1,0:T(8,128)}, bf16[512,2...) custom-call(bf16[512,1024]{1,0:T(8,128)(2,1)} %copy-done.13, ...), custom_call_target="tpu_custom_call" | custom-call | tf_op jit(solution)/shard_map/forward_last/pallas_call | solution.py:441
  302.4 75.3 %backward.2 = (bf16[512,1024]{1,0:T(8,128)(2,1)}, bf16[4,4,32,1024]{3,2,1,0:T(8,128)(2,1)}, bf16[512,256]{1,0:T(8,128)(2,1)}, bf16[1536,512]{1,0:T(8,128)(2,1)},...) custom-call(bf16[4,4,32,1024]{3,2,1,0:T(8,128)(2,1)} %bitcast.170, ...), custom_call_target="tpu_custom_call" | custom-call | tf_op jit(solution)/shard_map/backward/pallas_call | solution.py:585
  377.8 2.7 fusion.8
  380.5 4.9 fusion.5
  386.7 2.6 convert_dynamic-update-slice_fusion.1
  389.3 2.6 convert_dynamic-update-slice_fusion
  391.9 8.7 %copy.35 = bf16[1024,3072]{1,0:T(8,128)(2,1)} copy(bf16[1024,3072]{0,1:T(8,128)(2,1)} %convert_dynamic-update-slice_fusion) | data formatting | bytes 12582912 | tf_op jit(solution)/shard_map/concatenate | solution.py:809
  400.6 3.7 dynamic-slice_bitcast_fusion
  404.4 80.9 %backward.3 = (bf16[512,1024]{1,0:T(8,128)(2,1)}, bf16[4,4,32,1024]{3,2,1,0:T(8,128)(2,1)}, bf16[512,256]{1,0:T(8,128)(2,1)}, bf16[1536,512]{1,0:T(8,128)(2,1)},...) custom-call(bf16[4,4,32,1024]{3,2,1,0:T(8,128)(2,1)} %get-tuple-element.52.refs_0_, ...), custom_call_target="tpu_custom_call" | custom-call | tf_op jit(solution)/shard_map/backward/pallas_call | solution.py:585
  485.3 2.7 fusion.10
  488.0 4.9 fusion.6
  494.2 2.6 convert_dynamic-update-slice_fusion.3
  496.8 2.6 convert_dynamic-update-slice_fusion.2
  499.5 8.7 %copy.33 = bf16[1024,3072]{1,0:T(8,128)(2,1)} copy(bf16[1024,3072]{0,1:T(8,128)(2,1)} %convert_dynamic-update-slice_fusion.2) | data formatting | bytes 12582912 | tf_op jit(solution)/shard_map/concatenate | solution.py:809
  508.1 3.8 dynamic-slice_bitcast_fusion.1
  511.9 1.6 dynamic-slice_bitcast_fusion.7
  514.9 1.5 collective-permute-start.26
  516.5 2.4 bitcast_select_fusion.4
  518.8 20.9 %collective-permute-start.19 = (bf16[512,1024]{1,0:T(8,128)(2,1)}, bf16[512,1024]{1,0:T(8,128)(2,1)}, u32[]{:S(2)}, u32[]{:S(2)}) collective-permute-start(bf16[512,1024]{1,0:T(8,128)(2,1)} %bitcast_select_fusion.4), channel_id=1, source_target_pairs={{0,16},{16,0},{1,17},{17,1},{2,18},{18,2},{3,19},{19,3},{4,20},{20... | collective-permute-start | bytes 3145736 | tf_op jit(solution)/shard_map/ppermute | solution.py:877
  541.2 4.5 fusion
  548.3 3.1 fusion.1
  555.7 2.9 reshape.131
  558.6 4.9 constant_dynamic-slice_fusion.2
  563.4 3.5 copy.45
  567.0 2.9 copy.46
  569.8 14.9 %collective-permute-done.23 = bf16[256,3072]{1,0:T(8,128)(2,1)} collective-permute-done((bf16[256,3072]{1,0:T(8,128)(2,1)}, bf16[256,3072]{1,0:T(8,128)(2,1)}, u32[]{:S(2)}, u32[]{:S(2)}) %collective-permute-start.23) | collective-permute-done | bytes 1572896 | tf_op jit(solution)/shard_map/ppermute | solution.py:739
  584.7 3.6 fusion.3
  588.3 4.5 collective-permute-start.25
  592.8 24.9 %collective-permute-done.21 = bf16[256,3072]{1,0:T(8,128)(2,1)} collective-permute-done((bf16[256,3072]{1,0:T(8,128)(2,1)}, bf16[256,3072]{1,0:T(8,128)(2,1)}, u32[]{:S(2)}, u32[]{:S(2)}) %collective-permute-start.21) | collective-permute-done | bytes 1572896 | tf_op jit(solution)/shard_map/ppermute | solution.py:739
  617.7 3.2 fusion.2
  620.8 1.7 collective-permute-start.24
  628.3 1.6 maximum_bitcast_fusion
  629.9 3.4 collective-permute-done.28
  634.8 24.1 %collective-permute-done.24 = bf16[256,3072]{1,0:T(8,128)(2,1)} collective-permute-done((bf16[256,3072]{1,0:T(8,128)(2,1)}, bf16[256,3072]{1,0:T(8,128)(2,1)}, u32[]{:S(2)}, u32[]{:S(2)}) %collective-permute-start.24) | collective-permute-done | bytes 1572896 | tf_op jit(solution)/shard_map/ppermute | solution.py:823
  658.8 4.9 convert_add_fusion.4
  664.7 2.6 slice_bitcast_fusion
  671.4 10.3 %gather_sums.1 = f32[4,8,256]{2,1,0:T(8,128)} custom-call(f32[8,256]{1,0:T(8,128)} %select_maximum_fusion.x_ref), custom_call_target="tpu_custom_call" | custom-call | tf_op jit(solution)/shard_map/gather_sums/pallas_call | solution.py:663
  (194 shorter events, 53.6 us)
Async XLA Ops:
  0.6 47.3 %copy-start = (bf16[1,1024,1024]{2,1,0:T(8,128)(2,1)S(1)}, bf16[1,1024,1024]{2,1,0:T(8,128)(2,1)}, u32[]{:S(2)}) copy-start(bf16[1,1024,1024]{2,1,0:T(8,128)(2,1)} %param.27) | copy-start | bytes 6291460
  0.7 15.2 %copy-start.9 = (bf16[1,1,512,1024]{3,2,1,0:T(8,128)(2,1)S(1)}, bf16[1,1,512,1024]{3,2,1,0:T(8,128)(2,1)}, u32[]{:S(2)}) copy-start(bf16[1,1,512,1024]{3,2,1,0:T(8,128)(2,1)} %param.17) | copy-start | bytes 3145732
  2.1 54.8 %collective-permute-start.16 = (f32[2,1024]{1,0:T(2,128)}, f32[2,1024]{1,0:T(2,128)}, u32[]{:S(2)}, u32[]{:S(2)}) collective-permute-start(f32[2,1024]{1,0:T(2,128)} %pad_maximum_fusion.5), channel_id=1, source_target_pairs={{0,16},{16,0},{1,17},{17,1},{2,18},{18,2},{3,19},{19,3},{4,20},{20... | collective-permute-start | bytes 24584 | tf_op jit(solution)/shard_map/ppermute | solution.py:746
  6.7 44.3 %collective-permute-start.1 = (bf16[256,256]{1,0:T(8,128)(2,1)}, bf16[256,256]{1,0:T(8,128)(2,1)}, u32[]{:S(2)}, u32[]{:S(2)}) collective-permute-start(bf16[256,256]{1,0:T(8,128)(2,1)} %dynamic-slice_bitcast_fusion.10), channel_id=1, source_target_pairs={{0,16},{16,0},{1,17},{17,1},{2,18},{18,2},{3,19},{19,3},{4,20},{20... | collective-permute-start | bytes 393224 | tf_op jit(solution)/shard_map/ppermute | solution.py:716
  8.2 41.9 %collective-permute-start.7 = (bf16[64,1024]{1,0:T(8,128)(2,1)}, bf16[64,1024]{1,0:T(8,128)(2,1)}, u32[]{:S(2)}, u32[]{:S(2)}) collective-permute-start(bf16[64,1024]{1,0:T(8,128)(2,1)} %dynamic-slice_bitcast_fusion.9), channel_id=1, source_target_pairs={{0,16},{16,0},{1,17},{17,1},{2,18},{18,2},{3,19},{19,3},{4,20},{20... | collective-permute-start | bytes 393224 | tf_op jit(solution)/shard_map/ppermute | solution.py:716
  12.0 43.8 %collective-permute-start.4 = (bf16[256,512]{1,0:T(8,128)(2,1)}, bf16[256,512]{1,0:T(8,128)(2,1)}, u32[]{:S(2)}, u32[]{:S(2)}) collective-permute-start(bf16[256,512]{1,0:T(8,128)(2,1)} %fusion.15), channel_id=1, source_target_pairs={{0,16},{16,0},{1,17},{17,1},{2,18},{18,2},{3,19},{19,3},{4,20},{20... | collective-permute-start | bytes 786440 | tf_op jit(solution)/shard_map/ppermute | solution.py:716
  13.8 46.3 %collective-permute-start.13 = (bf16[256,1024]{1,0:T(8,128)(2,1)}, bf16[256,1024]{1,0:T(8,128)(2,1)}, u32[]{:S(2)}, u32[]{:S(2)}) collective-permute-start(bf16[256,1024]{1,0:T(8,128)(2,1)} %dynamic-slice_bitcast_fusion.4), channel_id=1, source_target_pairs={{0,16},{16,0},{1,17},{17,1},{2,18},{18,2},{3,19},{19,3},{4,20},{20... | collective-permute-start | bytes 1572872 | tf_op jit(solution)/shard_map/ppermute | solution.py:716
  15.8 3.7 copy-start.15
  49.0 8.5 %copy-start.30 = (f32[1,1024]{1,0:T(1,128)S(1)}, f32[1,1024]{1,0:T(1,128)}, u32[]{:S(2)}) copy-start(f32[1,1024]{1,0:T(1,128)} %param.23) | copy-start | bytes 12292
  49.1 8.5 %copy-start.31 = (f32[1,1024]{1,0:T(1,128)S(1)}, f32[1,1024]{1,0:T(1,128)}, u32[]{:S(2)}) copy-start(f32[1,1024]{1,0:T(1,128)} %param.18) | copy-start | bytes 12292
  50.2 2.3 collective-permute-start.8
  51.0 9.5 %copy-start.29 = (s32[1,512]{1,0:T(1,128)}, s32[1,512]{1,0:T(1,128)S(1)}, u32[]{:S(2)}) copy-start(s32[1,512]{1,0:T(1,128)S(1)} %get-tuple-element.142.refs_9_.refs_14_) | copy-start | bytes 6148
  51.0 3.2 collective-permute-start.2
  52.5 16.9 %collective-permute-start.10 = (bf16[256,1024]{1,0:T(8,128)(2,1)S(1)}, bf16[256,1024]{1,0:T(8,128)(2,1)S(1)}, u32[]{:S(2)}, u32[]{:S(2)}) collective-permute-start(bf16[256,1024]{1,0:T(8,128)(2,1)S(1)} %dynamic-slice_bitcast_fusion.5), channel_id=1, source_target_pairs={{0,16},{16,0},{1,17},{17,1},{2,18},{18,2},{3,19},{19,3},{4,20},{20... | collective-permute-start | bytes 1572872 | tf_op jit(solution)/shard_map/ppermute | solution.py:716
  54.1 9.3 %copy-start.25 = (bf16[512,1024]{1,0:T(8,128)(2,1)S(1)}, bf16[512,1024]{1,0:T(8,128)(2,1)}, u32[]{:S(2)}) copy-start(bf16[512,1024]{1,0:T(8,128)(2,1)} %bitcast_select_fusion.11) | copy-start | bytes 3145732
  54.2 9.2 %collective-permute-start.9 = (bf16[128,1024]{1,0:T(8,128)(2,1)S(1)}, bf16[128,1024]{1,0:T(8,128)(2,1)S(1)}, u32[]{:S(2)}, u32[]{:S(2)}) collective-permute-start(bf16[128,1024]{1,0:T(8,128)(2,1)S(1)} %get-tuple-element.104), channel_id=1, source_target_pairs={{0,8},{4,12},{8,0},{12,4},{1,9},{5,13},{9,1},{13,5},{2,10},{6,14},... | collective-permute-start | bytes 786440 | tf_op jit(solution)/shard_map/ppermute | solution.py:726
  55.8 3.1 collective-permute-start.5
  55.8 13.6 %copy-start.26 = (bf16[1,1024,256]{2,1,0:T(8,128)(2,1)S(1)}, bf16[1,1024,256]{2,1,0:T(8,128)(2,1)}, u32[]{:S(2)}) copy-start(bf16[1,1024,256]{2,1,0:T(8,128)(2,1)} %param.19) | copy-start | bytes 1572868
  56.9 10.9 %collective-permute-start.3 = (bf16[512,256]{1,0:T(8,128)(2,1)S(1)}, bf16[512,256]{1,0:T(8,128)(2,1)S(1)}, u32[]{:S(2)}, u32[]{:S(2)}) collective-permute-start(bf16[512,256]{1,0:T(8,128)(2,1)S(1)} %get-tuple-element.108), channel_id=1, source_target_pairs={{0,8},{4,12},{8,0},{12,4},{1,9},{5,13},{9,1},{13,5},{2,10},{6,14},... | collective-permute-start | bytes 786440 | tf_op jit(solution)/shard_map/ppermute | solution.py:726
  58.8 160.7 %collective-permute-start.17 = (bf16[512,1024]{1,0:T(8,128)(2,1)}, bf16[512,1024]{1,0:T(8,128)(2,1)}, u32[]{:S(2)}, u32[]{:S(2)}) collective-permute-start(bf16[512,1024]{1,0:T(8,128)(2,1)} %bitcast.2), channel_id=1, source_target_pairs={{16,0},{17,1},{18,2},{19,3},{20,4},{21,5},{22,6},{23,7},{24,8},{25... | collective-permute-start | bytes 3145736 | tf_op jit(solution)/shard_map/ppermute | solution.py:772
  60.1 10.4 %collective-permute-start.14 = (bf16[256,1024]{1,0:T(8,128)(2,1)}, bf16[256,1024]{1,0:T(8,128)(2,1)S(1)}, u32[]{:S(2)}, u32[]{:S(2)}) collective-permute-start(bf16[256,1024]{1,0:T(8,128)(2,1)} %collective-permute-done.13), channel_id=1, source_target_pairs={{0,4},{4,0},{8,12},{12,8},{1,5},{5,1},{9,13},{13,9},{2,6},{6,2},{1... | collective-permute-start | bytes 1572872 | tf_op jit(solution)/shard_map/ppermute | solution.py:717
  63.4 47.9 %collective-permute-start = (bf16[512,1024]{1,0:T(8,128)(2,1)S(1)}, bf16[512,1024]{1,0:T(8,128)(2,1)S(1)}, u32[]{:S(2)}, u32[]{:S(2)}) collective-permute-start(bf16[512,1024]{1,0:T(8,128)(2,1)S(1)} %copy-done.25), channel_id=1, source_target_pairs={{0,16},{16,0},{1,17},{17,1},{2,18},{18,2},{3,19},{19,3},{4,20},{20... | collective-permute-start | bytes 3145736 | tf_op jit(solution)/shard_map/ppermute | solution.py:771
  67.9 44.4 %collective-permute-start.6 = (bf16[512,512]{1,0:T(8,128)(2,1)S(1)}, bf16[512,512]{1,0:T(8,128)(2,1)S(1)}, u32[]{:S(2)}, u32[]{:S(2)}) collective-permute-start(bf16[512,512]{1,0:T(8,128)(2,1)S(1)} %get-tuple-element.106), channel_id=1, source_target_pairs={{0,8},{4,12},{8,0},{12,4},{1,9},{5,13},{9,1},{13,5},{2,10},{6,14},... | collective-permute-start | bytes 1572872 | tf_op jit(solution)/shard_map/ppermute | solution.py:726
  69.4 3.7 collective-permute-start.11
  72.5 44.3 %collective-permute-start.15 = (bf16[512,1024]{1,0:T(8,128)(2,1)S(1)}, bf16[512,1024]{1,0:T(8,128)(2,1)S(1)}, u32[]{:S(2)}, u32[]{:S(2)}) collective-permute-start(bf16[512,1024]{1,0:T(8,128)(2,1)S(1)} %get-tuple-element.100), channel_id=1, source_target_pairs={{0,8},{4,12},{8,0},{12,4},{1,9},{5,13},{9,1},{13,5},{2,10},{6,14},... | collective-permute-start | bytes 3145736 | tf_op jit(solution)/shard_map/ppermute | solution.py:726
  73.3 38.0 %copy-start.10 = (bf16[1,1,512,1024]{3,2,1,0:T(8,128)(2,1)S(1)}, bf16[1,1,512,1024]{3,2,1,0:T(8,128)(2,1)}, u32[]{:S(2)}) copy-start(bf16[1,1,512,1024]{3,2,1,0:T(8,128)(2,1)} %param.17) | copy-start | bytes 3145732
  73.3 38.0 %copy-start.11 = (bf16[341,1024]{1,0:T(8,128)(2,1)S(1)}, bf16[341,1024]{1,0:T(8,128)(2,1)}, u32[]{:S(2)}) copy-start(bf16[341,1024]{1,0:T(8,128)(2,1)} %slice_bitcast_fusion.2) | copy-start | bytes 2095108
  73.9 51.7 %collective-permute-start.12 = (bf16[512,1024]{1,0:T(8,128)(2,1)S(1)}, bf16[512,1024]{1,0:T(8,128)(2,1)S(1)}, u32[]{:S(2)}, u32[]{:S(2)}) collective-permute-start(bf16[512,1024]{1,0:T(8,128)(2,1)S(1)} %get-tuple-element.102), channel_id=1, source_target_pairs={{0,8},{4,12},{8,0},{12,4},{1,9},{5,13},{9,1},{13,5},{2,10},{6,14},... | collective-permute-start | bytes 3145736 | tf_op jit(solution)/shard_map/ppermute | solution.py:726
  112.1 3.8 copy-start.14
  112.1 4.6 copy-start.13
  377.8 2.7 copy-start.33
  380.5 4.9 copy-start.41
  380.5 4.9 copy-start.43
  380.5 6.2 copy-start.37
  380.5 6.2 copy-start.39
  404.4 136.9 %collective-permute-start.22 = (bf16[2,256,3072]{2,1,0:T(8,128)(2,1)}, bf16[2,256,3072]{2,1,0:T(8,128)(2,1)}, u32[]{:S(2)}, u32[]{:S(2)}) collective-permute-start(bf16[2,256,3072]{2,1,0:T(8,128)(2,1)} %dynamic-slice_bitcast_fusion), channel_id=1, source_target_pairs={{0,4},{4,0},{8,12},{12,8},{1,5},{5,1},{9,13},{13,9},{2,6},{6,2},{1... | collective-permute-start | bytes 9437192 | tf_op jit(solution)/shard_map/ppermute | solution.py:735
  485.3 2.7 copy-start.32
  488.0 4.9 copy-start.40
  488.0 4.9 copy-start.42
  488.0 6.2 copy-start.35
  488.0 6.2 copy-start.38
  508.1 5.4 copy-start.28
  511.9 36.4 %collective-permute-start.20 = (bf16[2,256,3072]{2,1,0:T(8,128)(2,1)}, bf16[2,256,3072]{2,1,0:T(8,128)(2,1)}, u32[]{:S(2)}, u32[]{:S(2)}) collective-permute-start(bf16[2,256,3072]{2,1,0:T(8,128)(2,1)} %dynamic-slice_bitcast_fusion.1), channel_id=1, source_target_pairs={{0,4},{4,0},{8,12},{12,8},{1,5},{5,1},{9,13},{13,9},{2,6},{6,2},{1... | collective-permute-start | bytes 9437192 | tf_op jit(solution)/shard_map/ppermute | solution.py:735
  513.6 26.1 %copy-start.6 = (bf16[4,4,32,1024]{3,2,1,0:T(8,128)(2,1)S(1)}, bf16[4,4,32,1024]{3,2,1,0:T(8,128)(2,1)}, u32[]{:S(2)}) copy-start(bf16[4,4,32,1024]{3,2,1,0:T(8,128)(2,1)} %get-tuple-element.44.refs_2_.refs_1_) | copy-start | bytes 3145732
  513.6 26.1 %copy-start.24 = (bf16[4,4,32,1024]{3,2,1,0:T(8,128)(2,1)S(1)}, bf16[4,4,32,1024]{3,2,1,0:T(8,128)(2,1)}, u32[]{:S(2)}) copy-start(bf16[4,4,32,1024]{3,2,1,0:T(8,128)(2,1)} %get-tuple-element.46) | copy-start | bytes 3145732
  514.9 38.7 %collective-permute-start.26 = (bf16[171,256]{1,0:T(8,128)(2,1)S(1)}, bf16[171,256]{1,0:T(8,128)(2,1)S(1)}, u32[]{:S(2)}, u32[]{:S(2)}) collective-permute-start(bf16[171,256]{1,0:T(8,128)(2,1)S(1)} %constant_dynamic-slice_fusion.3), channel_id=1, source_target_pairs={{16,0},{17,1},{18,2},{19,3},{20,4},{21,5},{22,6},{23,7},{24,8},{25... | collective-permute-start | bytes 262664 | tf_op jit(solution)/shard_map/ppermute | solution.py:830
  518.8 105.2 %collective-permute-start.19 = (bf16[512,1024]{1,0:T(8,128)(2,1)}, bf16[512,1024]{1,0:T(8,128)(2,1)}, u32[]{:S(2)}, u32[]{:S(2)}) collective-permute-start(bf16[512,1024]{1,0:T(8,128)(2,1)} %bitcast_select_fusion.4), channel_id=1, source_target_pairs={{0,16},{16,0},{1,17},{17,1},{2,18},{18,2},{3,19},{19,3},{4,20},{20... | collective-permute-start | bytes 3145736 | tf_op jit(solution)/shard_map/ppermute | solution.py:877
  539.7 8.5 %slice-start = ((s8[6291456]{0:T(1024)(128)(4,1)}), s8[4194304]{0:T(1024)(128)(4,1)S(1)}, s32[]{:S(2)}) async-start(s8[6291456]{0:T(1024)(128)(4,1)} %bitcast.164), calls=%async_computation | async-start | bytes 8388608
  541.2 7.1 %slice-start.1 = ((s8[6291456]{0:T(1024)(128)(4,1)}), s8[2097152]{0:T(1024)(128)(4,1)S(1)}, s32[]{:S(2)}) async-start(s8[6291456]{0:T(1024)(128)(4,1)} %bitcast.164), calls=%async_computation.1 | async-start | bytes 4194304
  541.2 84.2 %collective-permute-start.18 = (bf16[512,1024]{1,0:T(8,128)(2,1)}, bf16[512,1024]{1,0:T(8,128)(2,1)}, u32[]{:S(2)}, u32[]{:S(2)}) collective-permute-start(bf16[512,1024]{1,0:T(8,128)(2,1)} %bitcast.22), channel_id=1, source_target_pairs={{0,16},{16,0},{1,17},{17,1},{2,18},{18,2},{3,19},{19,3},{4,20},{20... | collective-permute-start | bytes 3145736 | tf_op jit(solution)/shard_map/ppermute | solution.py:877
  545.8 5.6 copy-start.2
  547.1 37.6 %collective-permute-start.23 = (bf16[256,3072]{1,0:T(8,128)(2,1)}, bf16[256,3072]{1,0:T(8,128)(2,1)}, u32[]{:S(2)}, u32[]{:S(2)}) collective-permute-start(bf16[256,3072]{1,0:T(8,128)(2,1)} %dynamic-slice_bitcast_fusion.2), channel_id=1, source_target_pairs={{0,8},{4,12},{8,0},{12,4},{1,9},{5,13},{9,1},{13,5},{2,10},{6,14},... | collective-permute-start | bytes 4718600 | tf_op jit(solution)/shard_map/ppermute | solution.py:739
  551.4 2.9 copy-start.3
  552.8 64.9 %collective-permute-start.21 = (bf16[256,3072]{1,0:T(8,128)(2,1)}, bf16[256,3072]{1,0:T(8,128)(2,1)}, u32[]{:S(2)}, u32[]{:S(2)}) collective-permute-start(bf16[256,3072]{1,0:T(8,128)(2,1)} %dynamic-slice_bitcast_fusion.3), channel_id=1, source_target_pairs={{0,8},{4,12},{8,0},{12,4},{1,9},{5,13},{9,1},{13,5},{2,10},{6,14},... | collective-permute-start | bytes 4718600 | tf_op jit(solution)/shard_map/ppermute | solution.py:739
  563.4 3.5 copy-start.12
  569.8 47.8 %copy-start.4 = (bf16[2,256,3072]{2,1,0:T(8,128)(2,1)S(1)}, bf16[2,256,3072]{2,1,0:T(8,128)(2,1)}, u32[]{:S(2)}) copy-start(bf16[2,256,3072]{2,1,0:T(8,128)(2,1)} %copy-done.3) | copy-start | bytes 9437188
  569.8 52.7 %collective-permute-start.27 = (bf16[2,256,768]{2,1,0:T(8,128)(2,1)}, bf16[2,256,768]{2,1,0:T(8,128)(2,1)S(1)}, u32[]{:S(2)}, u32[]{:S(2)}) collective-permute-start(bf16[2,256,768]{2,1,0:T(8,128)(2,1)} %bitcast.183), channel_id=1, source_target_pairs={{0,4},{4,0},{8,12},{12,8},{1,5},{5,1},{9,13},{13,9},{2,6},{6,2},{1... | collective-permute-start | bytes 2359304 | tf_op jit(solution)/shard_map/ppermute | solution.py:735
  588.3 46.5 %collective-permute-start.25 = (bf16[256,3072]{1,0:T(8,128)(2,1)}, bf16[256,3072]{1,0:T(8,128)(2,1)}, u32[]{:S(2)}, u32[]{:S(2)}) collective-permute-start(bf16[256,3072]{1,0:T(8,128)(2,1)} %fusion.3), channel_id=1, source_target_pairs={{0,16},{1,17},{2,18},{3,19},{4,20},{5,21},{6,22},{7,23},{8,24},{9,... | collective-permute-start | bytes 4718600 | tf_op jit(solution)/shard_map/ppermute | solution.py:823
  620.8 3.2 copy-start.8
  620.8 3.2 copy-start.20
  620.8 38.0 %collective-permute-start.24 = (bf16[256,3072]{1,0:T(8,128)(2,1)}, bf16[256,3072]{1,0:T(8,128)(2,1)}, u32[]{:S(2)}, u32[]{:S(2)}) collective-permute-start(bf16[256,3072]{1,0:T(8,128)(2,1)} %fusion.2), channel_id=1, source_target_pairs={{16,0},{17,1},{18,2},{19,3},{20,4},{21,5},{22,6},{23,7},{24,8},{25... | collective-permute-start | bytes 4718600 | tf_op jit(solution)/shard_map/ppermute | solution.py:823
  622.8 10.5 %collective-permute-start.28 = (bf16[256,768]{1,0:T(8,128)(2,1)S(1)}, bf16[256,768]{1,0:T(8,128)(2,1)S(1)}, u32[]{:S(2)}, u32[]{:S(2)}) collective-permute-start(bf16[256,768]{1,0:T(8,128)(2,1)S(1)} %dynamic-slice_bitcast_fusion.6), channel_id=1, source_target_pairs={{0,8},{4,12},{8,0},{12,4},{1,9},{5,13},{9,1},{13,5},{2,10},{6,14},... | collective-permute-start | bytes 1179656 | tf_op jit(solution)/shard_map/ppermute | solution.py:739
  663.7 3.6 copy-start.5
  664.7 18.4 %copy-start.1 = (bf16[1,1024,1024]{2,1,0:T(8,128)(2,1)S(1)}, bf16[1,1024,1024]{2,1,0:T(8,128)(2,1)}, u32[]{:S(2)}) copy-start(bf16[1,1024,1024]{2,1,0:T(8,128)(2,1)} %param.27) | copy-start | bytes 6291460
  (12 other events, 25.7 us)
